TPU v7x, 512 devices: a whole 4x4x16 slice. The times are simulated.
512 devices in a mesh: section: 8 (over x, z_hi), ctx: 32 (over z_lo, y), tp: 2 (over core).
Axes of the slice: x: 4, y: 4, z: 16 (z_hi: 2, z_lo: 8; z = z_hi * 8 + z_lo), core: 2. Of those that a mesh axis runs over, the one named last changes fastest.
Arguments:
- queries: bfloat16 [8, 2, 4096, 4096], P('section', None, 'ctx', 'tp'), may hold values from -48 to 48
- keyvals: bfloat16 [8, 2, 2, 4096, 512], P('section', None, None, ('ctx', 'tp')), may hold values from -4 to 4
- segments: int32 [8, 2, 4096], P('section', None, 'ctx'), may hold values from 0 to 3, never falling along the last dimension, each value on 1 to 3072 neighbouring positions
Outputs:
- handed: bfloat16 [8, 2, 4096, 4096], P('section', None, 'ctx', 'tp')
Inputs may be any that keep to these rules, and one draw needn't show every extreme that they name: `segments`: document numbers never fall along a stream; each document is at most 3072 positions long, and one is exactly that long.
All inputs are finite; a program needn't handle non-finite values.
Results may differ from a plain program's by a relative error of at most 0.0035.
Values may be sent and summed in bfloat16 or wider, within the bound.
No kernel may reach another device: no remote copies, remote signals or barrier semaphores. Data moves between devices by JAX's collectives and lax.ppermute only.
A program may use at most 128 MiB of HBM per device.

v0:
```python
import functools
import math

import jax
import jax.numpy as jnp
from jax import lax
from jax.experimental import pallas as pl
from jax.experimental.pallas import tpu as pltpu
from jax.sharding import Mesh
from jax.sharding import PartitionSpec as P

HD = 128
KVH = 4
GROUPS = 8
ROWS = 8
YS = 4
PIECE = 64
CHUNK = 2 * PIECE + 16
BACK = 6
MASKED = -1e30


def attend_kernel(offset, last, place, query_docs, key_part, value_part, *refs):
    if offset:
        queries, *refs = refs
    if offset == 0:
        blocks, refs = refs[:YS], refs[YS:]
        (queries, max_ref, sum_ref, acc_ref, even, odd) = refs
        for turn, block in enumerate(blocks):
            home = lax.rem(place[2] + YS - turn, YS)
            queries[pl.ds(pl.multiple_of(home * HD, HD), HD), :] = block[...]
        old_max_ref = old_sum_ref = old_acc_ref = None
    elif last:
        (old_max_ref, old_sum_ref, old_acc_ref, _, out_ref) = refs[:5]
        (max_ref, sum_ref, acc_ref, even, odd) = refs[5:]
    else:
        (old_max_ref, old_sum_ref, old_acc_ref) = refs[:3]
        (max_ref, sum_ref, acc_ref, even, odd) = refs[3:]
    span = queries.shape[0]
    heads = queries.shape[1] // HD
    rate = math.log2(math.e) / math.sqrt(HD)
    docs = query_docs[0:1, :]

    def fold(masked):
        keys = key_part[:span, :]
        values = value_part[...]
        if masked:
            key_docs = key_part[span : span + YS, :].astype(jnp.float32)
            start = jnp.zeros((1, span), jnp.float32)
            for doc in range(1, 4):
                below = jnp.sum((key_docs < doc).astype(jnp.float32))
                start = jnp.where(docs == doc, below, start)
            start = start.astype(jnp.int32)

        def score(head):
            columns = pl.ds(pl.multiple_of(head * HD, HD), HD)
            return lax.dot_general(
                keys,
                queries[:, columns],
                (((1,), (1,)), ((), ())),
                preferred_element_type=jnp.float32,
            )

        def one_head(head, scores):
            if masked:
                key_pos = lax.broadcasted_iota(jnp.int32, (span, span), 0)
                allowed = key_pos >= start
                if offset == 0:
                    query_pos = lax.broadcasted_iota(jnp.int32, (span, span), 1)
                    allowed = allowed & (key_pos <= query_pos)
                scores = jnp.where(allowed, scores, MASKED)
            top = jnp.max(scores, axis=0, keepdims=True)
            if offset:
                old_max = old_max_ref[pl.ds(head, 1), :]
                top = jnp.maximum(old_max, top)
            terms = jnp.exp2((scores - top) * rate)
            total = jnp.sum(terms, axis=0, keepdims=True)
            product = lax.dot_general(
                values,
                terms.astype(jnp.bfloat16),
                (((0,), (0,)), ((), ())),
                preferred_element_type=jnp.float32,
            )
            if offset:
                factor = jnp.exp2((old_max - top) * rate)
                total = total + factor * old_sum_ref[pl.ds(head, 1), :]
                product = product + factor * old_acc_ref[head]
            max_ref[pl.ds(head, 1), :] = top
            sum_ref[pl.ds(head, 1), :] = total
            acc_ref[head] = product

        def two_heads(pair, _):
            odd[...] = score(2 * pair + 1)
            one_head(2 * pair, even[...])
            even[...] = score(jnp.minimum(2 * pair + 2, heads - 1))
            one_head(2 * pair + 1, odd[...])
            return 0

        even[...] = score(0)
        lax.fori_loop(0, heads // 2, two_heads, 0)

    if offset == 0:
        fold(True)
    else:
        key_docs = key_part[span : span + YS, :].astype(jnp.float32)
        low = jnp.min(key_docs)
        first_doc = jnp.min(docs)
        last_doc = jnp.max(docs)
        live = (place[0] >= offset) & (jnp.max(key_docs) >= first_doc)
        pl.when(live & (low >= last_doc))(functools.partial(fold, False))
        pl.when(live & (low < last_doc))(functools.partial(fold, True))

        @pl.when(jnp.logical_not(live))
        def _():
            for source, target in zip(
                (old_max_ref, old_sum_ref, old_acc_ref), (max_ref, sum_ref, acc_ref)
            ):
                target[...] = source[...]

    if last:

        def one_result(head, _):
            columns = pl.ds(pl.multiple_of(head * HD, HD), HD)
            scaled = acc_ref[head] / sum_ref[pl.ds(head, 1), :]
            rows = jnp.transpose(scaled).astype(out_ref.dtype)
            for block in range(YS):
                slot = lax.rem(block + place[1], YS)
                out_ref[slot, :, columns] = rows[block * HD : (block + 1) * HD, :]
            return 0

        lax.fori_loop(0, heads, one_result, 0)


def attend(place, query_docs, parts, offset, held, last):
    span = YS * HD
    width = GROUPS * HD
    state_shapes = [
        jax.ShapeDtypeStruct((GROUPS, span), jnp.float32),
        jax.ShapeDtypeStruct((GROUPS, span), jnp.float32),
        jax.ShapeDtypeStruct((GROUPS, HD, span), jnp.float32),
    ]
    operands = [place, query_docs, *parts, *held]
    vmem = pl.BlockSpec(memory_space=pltpu.VMEM)
    scratch = [pltpu.VMEM((span, span), jnp.float32)] * 2
    out_shape = state_shapes
    if last:
        out_shape = [jax.ShapeDtypeStruct((YS, span // YS, width), jnp.bfloat16)]
        scratch = [pltpu.VMEM(s.shape, s.dtype) for s in state_shapes] + scratch
    elif offset == 0:
        out_shape = [jax.ShapeDtypeStruct((span, width), jnp.bfloat16)] + state_shapes
    return pl.pallas_call(
        functools.partial(attend_kernel, offset, last),
        out_shape=out_shape,
        in_specs=[pl.BlockSpec(memory_space=pltpu.SMEM)] + [vmem] * (len(operands) - 1),
        out_specs=[vmem] * len(out_shape),
        scratch_shapes=scratch,
        cost_estimate=pl.CostEstimate(
            flops=4 * GROUPS * span * span * HD,
            transcendentals=GROUPS * span * span,
            bytes_accessed=2 * span * width + 8 * GROUPS * HD * span,
        ),
        compiler_params=pltpu.CompilerParams(vmem_limit_bytes=32 << 20),
        name="attend",
    )(*operands)


def local(queries, keyvals, segments):
    section = lax.axis_index("section")
    row = lax.axis_index("row")
    y = lax.axis_index("y")
    core = lax.axis_index("core")

    source = queries[0]
    blocks = []
    for turn in range(YS):
        route = []
        for a in range(YS):
            for half in range(2):
                job = (a + turn) % YS
                route.append((2 * a + half, 2 * (2 * half + job // 2) + job % 2))
        job = (y + turn) % YS
        block = lax.dynamic_slice(
            source, (job % 2, 0, (job // 2) * GROUPS * HD), (1, HD, GROUPS * HD)
        )
        blocks.append(lax.ppermute(block[0], ("y", "core"), route))

    pieces = keyvals[0].reshape(2, 2, PIECE, KVH, HD).transpose(3, 0, 1, 2, 4)
    pieces = pieces.reshape(8, 2 * PIECE, HD)
    docs = segments[0].astype(jnp.bfloat16)
    docs = lax.dynamic_slice_in_dim(docs, core * PIECE, PIECE, 1)
    docs = jnp.pad(docs, ((0, 0), (0, HD - PIECE)), constant_values=9)
    docs = jnp.broadcast_to(docs[None, :, None, :], (KVH, 2, 16, HD)).reshape(8, 16, HD)
    message = jnp.concatenate([pieces, docs], axis=1)
    message = lax.all_to_all(message, ("y", "core"), 0, 0, tiled=True)

    docs = message[:, 2 * PIECE, :PIECE].reshape(YS, HD)
    key_part = jnp.concatenate(
        [message[:, :PIECE].reshape(YS * HD, HD), jnp.pad(docs, ((0, 16 - YS), (0, 0)))]
    )
    value_part = message[:, PIECE : 2 * PIECE].reshape(YS * HD, HD)
    query_docs = jnp.broadcast_to(docs.reshape(1, YS * HD).astype(jnp.float32), (8, YS * HD))
    goal = jnp.where(
        (section == 7) & (core == 0), 1, jnp.where((section == 0) & (core == 1), 0, core)
    )
    base = 2 * (y % 2) + goal
    place = jnp.stack([row, (YS - base) % YS, 2 * (y % 2) + core]).astype(jnp.int32)

    def hop(part, step):
        route = [(a, a + 1) for a in range(step - 1, ROWS - 1)]
        return tuple(lax.ppermute(x, "row", route) for x in part)

    own_part = (key_part, value_part)
    part = hop(own_part, 1)
    own, *state = attend(place, query_docs, own_part, 0, blocks, False)
    token = None
    for step in range(1, BACK + 1):
        if step < BACK:
            keys, state = lax.optimization_barrier((part[0], state))
            part = (keys, part[1])
            later = hop(part, step + 1)
        if step == BACK - 1:
            token = lax.ppermute(part[0][YS * HD :], "row", [(7, 3), (6, 2), (5, 4)])
            token = token + lax.ppermute(token, "row", [(3, 1), (2, 0)])
        held = [own, *state] + ([token] if step == BACK else [])
        state = attend(place, query_docs, part, step, held, step == BACK)
        part = later
    out = state[0]

    received = []
    for turn in range(YS):
        route = []
        for s in range(8):
            for head in range(YS):
                for stream in range(2):
                    s_to = s + 1 - 2 * stream
                    slot = stream
                    if s_to < 0 or s_to > 7:
                        s_to, slot = s, 1 - stream
                    block = (2 * (head % 2) + slot + turn) % YS
                    route.append(((s * YS + head) * 2 + stream, (s_to * YS + block) * 2 + head // 2))
        received.append(lax.ppermute(out[turn], ("section", "y", "core"), route))
    stacked = jnp.stack(received)
    parts = [
        lax.dynamic_index_in_dim(stacked, (y - v) % YS, 0, keepdims=False) for v in range(YS)
    ]
    slots = [jnp.concatenate([parts[slot], parts[2 + slot]], axis=1) for slot in range(2)]
    return jnp.stack(slots)[None]


def solution(mesh):
    grid = Mesh(mesh.devices.reshape(8, ROWS, YS, 2), ("section", "row", "y", "core"))
    return jax.shard_map(
        local,
        mesh=grid,
        in_specs=(
            P("section", None, ("row", "y"), "core"),
            P("section", None, None, ("row", "y", "core"), None),
            P("section", None, ("row", "y")),
        ),
        out_specs=P("section", None, ("row", "y"), "core"),
        check_vma=False,
    )
```

profile of v0, /device:TPU:3, one launch (start us, length us, event | category | flops | bytes accessed | tf_op | source)
XLA Modules:
  0.0 191.1 jit_solution(9358771010051890285)
XLA Ops:
  0.0 0.8 convert_element_type.19
  0.8 1.0 reshape_squeeze.6
  1.9 0.7 pad_maximum_fusion.1
  2.7 5.1 %all-to-all-start = ((bf16[8,144,128]{2,1,0:T(8,128)(2,1)}), bf16[8,144,128]{2,1,0:T(8,128)(2,1)S(1)}, u32[]{:S(2)}, u32[]{:S(2)}) async-start(bf16[8,144,128]{2,1,0:T(8,128)(2,1)} %pad_maximum_fusion.1), calls=%async_computation | async-start | bytes 589824 | tf_op jit(solution)/shard_map/all_to_all | solution.py:194
  7.9 5.0 %collective-permute-start.1 = (bf16[128,1024]{1,0:T(8,128)(2,1)S(1)}, bf16[128,1024]{1,0:T(8,128)(2,1)S(1)}, u32[]{:S(2)}, u32[]{:S(2)}) collective-permute-start(bf16[128,1024]{1,0:T(8,128)(2,1)S(1)} %get-tuple-element.93), channel_id=1, source_target_pairs={{0,0},{1,4},{2,1},{3,5},{4,2},{5,6},{6,3},{7,7},{8,8},{9,12},{10,9... | collective-permute-start | bytes 786440 | tf_op jit(solution)/shard_map/ppermute | solution.py:185
  13.0 2.8 %collective-permute-start.2 = (bf16[128,1024]{1,0:T(8,128)(2,1)S(1)}, bf16[128,1024]{1,0:T(8,128)(2,1)S(1)}, u32[]{:S(2)}, u32[]{:S(2)}) collective-permute-start(bf16[128,1024]{1,0:T(8,128)(2,1)S(1)} %get-tuple-element.92), channel_id=1, source_target_pairs={{0,1},{1,5},{2,2},{3,6},{4,3},{5,7},{6,0},{7,4},{8,9},{9,13},{10,1... | collective-permute-start | bytes 786440 | tf_op jit(solution)/shard_map/ppermute | solution.py:185
  15.8 2.0 %collective-permute-start.3 = (bf16[128,1024]{1,0:T(8,128)(2,1)S(1)}, bf16[128,1024]{1,0:T(8,128)(2,1)S(1)}, u32[]{:S(2)}, u32[]{:S(2)}) collective-permute-start(bf16[128,1024]{1,0:T(8,128)(2,1)S(1)} %get-tuple-element.94), channel_id=1, source_target_pairs={{0,2},{1,6},{2,3},{3,7},{4,0},{5,4},{6,1},{7,5},{8,10},{9,14},{10,... | collective-permute-start | bytes 786440 | tf_op jit(solution)/shard_map/ppermute | solution.py:185
  17.7 2.2 %collective-permute-start.4 = (bf16[128,1024]{1,0:T(8,128)(2,1)S(1)}, bf16[128,1024]{1,0:T(8,128)(2,1)S(1)}, u32[]{:S(2)}, u32[]{:S(2)}) collective-permute-start(bf16[128,1024]{1,0:T(8,128)(2,1)S(1)} %get-tuple-element.91), channel_id=1, source_target_pairs={{0,3},{1,7},{2,0},{3,4},{4,1},{5,5},{6,2},{7,6},{8,11},{9,15},{10,... | collective-permute-start | bytes 786440 | tf_op jit(solution)/shard_map/ppermute | solution.py:185
  20.2 3.5 %collective-permute-start = (bf16[528,128]{1,0:T(8,128)(2,1)S(1)}, bf16[528,128]{1,0:T(8,128)(2,1)S(1)}, u32[]{:S(2)}, u32[]{:S(2)}) collective-permute-start(bf16[528,128]{1,0:T(8,128)(2,1)S(1)} %fusion.1.key_part), channel_id=1, source_target_pairs={{0,8},{8,16},{16,24},{24,32},{32,40},{40,48},{48,56},{1,9},{9,17},... | collective-permute-start | bytes 405512 | tf_op jit(solution)/shard_map/ppermute | solution.py:210
  23.7 3.5 %collective-permute-start.6 = (bf16[512,128]{1,0:T(8,128)(2,1)S(1)}, bf16[512,128]{1,0:T(8,128)(2,1)S(1)}, u32[]{:S(2)}, u32[]{:S(2)}) collective-permute-start(bf16[512,128]{1,0:T(8,128)(2,1)S(1)} %bitcast.47), channel_id=1, source_target_pairs={{0,8},{8,16},{16,24},{24,32},{32,40},{40,48},{48,56},{1,9},{9,17},... | collective-permute-start | bytes 393224 | tf_op jit(solution)/shard_map/ppermute | solution.py:210
  27.4 2.7 %collective-permute-done.3.refs_2_ = bf16[128,1024]{1,0:T(8,128)(2,1)S(1)} collective-permute-done((bf16[128,1024]{1,0:T(8,128)(2,1)S(1)}, bf16[128,1024]{1,0:T(8,128)(2,1)S(1)}, u32[]{:S(2)}, u32[]{:S(2)}) %collective-permute-start.3) | collective-permute-done | bytes 262176 | tf_op jit(solution)/shard_map/ppermute | solution.py:185
  30.1 4.6 %attend.7 = (bf16[512,1024]{1,0:T(8,128)(2,1)S(1)}, f32[8,512]{1,0:T(8,128)S(1)}, f32[8,512]{1,0:T(8,128)S(1)}, f32[8,128,512]{2,1,0:T(8,128)S(1)}) custom-call(s32[3]{0:T(128)S(1)} %pad_add_fusion.place, f32[8,512]{1,0:T(8,128)S(1)} %broadcast_in_dim.21.query_docs, bf16[528,128]{1,0:T(8,128)(2,1)S(1)} %fusion.1.key_part, bf16[512,128]{1,0:T(8,128)(2,1)S(1)} %bitcast.48, ...), custom_call_target="tpu_custom_call" | custom-call | flops 1073741824 | bytes 5242880 | tf_op jit(solution)/shard_map/attend/pallas_call | solution.py:151
  34.7 0.7 collective-permute-start.5
  36.0 0.8 attend.8
  36.9 0.7 collective-permute-start.7
  38.2 0.8 attend.9
  40.4 0.8 attend.10
  41.3 0.7 collective-permute-start.11
  42.6 0.8 attend.11
  45.5 1.5 collective-permute-start.17
  47.0 0.8 attend.12
  47.8 43.5 %collective-permute-done.17 = bf16[16,128]{1,0:T(8,128)(2,1)S(1)} collective-permute-done((bf16[16,128]{1,0:T(8,128)(2,1)S(1)}, bf16[16,128]{1,0:T(8,128)(2,1)S(1)}, u32[]{:S(2)}, u32[]{:S(2)}) %collective-permute-start.17) | collective-permute-done | bytes 4128 | tf_op jit(solution)/shard_map/ppermute | solution.py:223
  91.3 1.9 attend.13
  93.3 3.7 %collective-permute-start.18 = (bf16[128,1024]{1,0:T(8,128)(2,1)S(1)}, bf16[128,1024]{1,0:T(8,128)(2,1)S(1)}, u32[]{:S(2)}, u32[]{:S(2)}) collective-permute-start(bf16[128,1024]{1,0:T(8,128)(2,1)S(1)} %get-tuple-element.87), channel_id=1, source_target_pairs={{0,64},{1,0},{2,68},{3,4},{4,65},{5,1},{6,69},{7,5},{64,128},{65,2... | collective-permute-start | bytes 786440 | tf_op jit(solution)/shard_map/ppermute | solution.py:241
  97.0 13.9 %collective-permute-start.19 = (bf16[128,1024]{1,0:T(8,128)(2,1)S(1)}, bf16[128,1024]{1,0:T(8,128)(2,1)S(1)}, u32[]{:S(2)}, u32[]{:S(2)}) collective-permute-start(bf16[128,1024]{1,0:T(8,128)(2,1)S(1)} %get-tuple-element.90), channel_id=1, source_target_pairs={{0,66},{1,2},{2,70},{3,6},{4,67},{5,3},{6,71},{7,7},{64,130},{65,4... | collective-permute-start | bytes 786440 | tf_op jit(solution)/shard_map/ppermute | solution.py:241
  110.9 1.9 %collective-permute-start.20 = (bf16[128,1024]{1,0:T(8,128)(2,1)S(1)}, bf16[128,1024]{1,0:T(8,128)(2,1)S(1)}, u32[]{:S(2)}, u32[]{:S(2)}) collective-permute-start(bf16[128,1024]{1,0:T(8,128)(2,1)S(1)} %get-tuple-element.89), channel_id=1, source_target_pairs={{0,68},{1,4},{2,64},{3,0},{4,69},{5,5},{6,65},{7,1},{64,132},{65,6... | collective-permute-start | bytes 786440 | tf_op jit(solution)/shard_map/ppermute | solution.py:241
  112.8 10.8 %collective-permute-start.21 = (bf16[128,1024]{1,0:T(8,128)(2,1)S(1)}, bf16[128,1024]{1,0:T(8,128)(2,1)S(1)}, u32[]{:S(2)}, u32[]{:S(2)}) collective-permute-start(bf16[128,1024]{1,0:T(8,128)(2,1)S(1)} %get-tuple-element.88), channel_id=1, source_target_pairs={{0,70},{1,6},{2,66},{3,2},{4,71},{5,7},{6,67},{7,3},{64,134},{65,0... | collective-permute-start | bytes 786440 | tf_op jit(solution)/shard_map/ppermute | solution.py:241
  123.7 32.9 %collective-permute-done.18 = bf16[128,1024]{1,0:T(8,128)(2,1)S(1)} collective-permute-done((bf16[128,1024]{1,0:T(8,128)(2,1)S(1)}, bf16[128,1024]{1,0:T(8,128)(2,1)S(1)}, u32[]{:S(2)}, u32[]{:S(2)}) %collective-permute-start.18) | collective-permute-done | bytes 262176 | tf_op jit(solution)/shard_map/ppermute | solution.py:241
  156.6 7.6 %collective-permute-done.19 = bf16[128,1024]{1,0:T(8,128)(2,1)S(1)} collective-permute-done((bf16[128,1024]{1,0:T(8,128)(2,1)S(1)}, bf16[128,1024]{1,0:T(8,128)(2,1)S(1)}, u32[]{:S(2)}, u32[]{:S(2)}) %collective-permute-start.19) | collective-permute-done | bytes 262176 | tf_op jit(solution)/shard_map/ppermute | solution.py:241
  164.2 7.5 %collective-permute-done.20 = bf16[128,1024]{1,0:T(8,128)(2,1)S(1)} collective-permute-done((bf16[128,1024]{1,0:T(8,128)(2,1)S(1)}, bf16[128,1024]{1,0:T(8,128)(2,1)S(1)}, u32[]{:S(2)}, u32[]{:S(2)}) %collective-permute-start.20) | collective-permute-done | bytes 262176 | tf_op jit(solution)/shard_map/ppermute | solution.py:241
  171.7 17.9 %collective-permute-done.21 = bf16[128,1024]{1,0:T(8,128)(2,1)S(1)} collective-permute-done((bf16[128,1024]{1,0:T(8,128)(2,1)S(1)}, bf16[128,1024]{1,0:T(8,128)(2,1)S(1)}, u32[]{:S(2)}, u32[]{:S(2)}) %collective-permute-start.21) | collective-permute-done | bytes 262176 | tf_op jit(solution)/shard_map/ppermute | solution.py:241
  190.0 1.1 maximum_bitcast_fusion
  (47 shorter events, 6.3 us)
Async XLA Ops:
  0.0 7.8 %copy-start = (bf16[1,2,128,2048]{3,2,1,0:T(8,128)(2,1)S(1)}, bf16[1,2,128,2048]{3,2,1,0:T(8,128)(2,1)}, u32[]{:S(2)}) copy-start(bf16[1,2,128,2048]{3,2,1,0:T(8,128)(2,1)} %param.3) | copy-start | bytes 3145732
  2.7 17.3 %all-to-all-start = ((bf16[8,144,128]{2,1,0:T(8,128)(2,1)}), bf16[8,144,128]{2,1,0:T(8,128)(2,1)S(1)}, u32[]{:S(2)}, u32[]{:S(2)}) async-start(bf16[8,144,128]{2,1,0:T(8,128)(2,1)} %pad_maximum_fusion.1), calls=%async_computation | async-start | bytes 589824 | tf_op jit(solution)/shard_map/all_to_all | solution.py:194
  7.9 15.8 %collective-permute-start.1 = (bf16[128,1024]{1,0:T(8,128)(2,1)S(1)}, bf16[128,1024]{1,0:T(8,128)(2,1)S(1)}, u32[]{:S(2)}, u32[]{:S(2)}) collective-permute-start(bf16[128,1024]{1,0:T(8,128)(2,1)S(1)} %get-tuple-element.93), channel_id=1, source_target_pairs={{0,0},{1,4},{2,1},{3,5},{4,2},{5,6},{6,3},{7,7},{8,8},{9,12},{10,9... | collective-permute-start | bytes 786440 | tf_op jit(solution)/shard_map/ppermute | solution.py:185
  13.0 14.4 %collective-permute-start.2 = (bf16[128,1024]{1,0:T(8,128)(2,1)S(1)}, bf16[128,1024]{1,0:T(8,128)(2,1)S(1)}, u32[]{:S(2)}, u32[]{:S(2)}) collective-permute-start(bf16[128,1024]{1,0:T(8,128)(2,1)S(1)} %get-tuple-element.92), channel_id=1, source_target_pairs={{0,1},{1,5},{2,2},{3,6},{4,3},{5,7},{6,0},{7,4},{8,9},{9,13},{10,1... | collective-permute-start | bytes 786440 | tf_op jit(solution)/shard_map/ppermute | solution.py:185
  15.8 14.3 %collective-permute-start.3 = (bf16[128,1024]{1,0:T(8,128)(2,1)S(1)}, bf16[128,1024]{1,0:T(8,128)(2,1)S(1)}, u32[]{:S(2)}, u32[]{:S(2)}) collective-permute-start(bf16[128,1024]{1,0:T(8,128)(2,1)S(1)} %get-tuple-element.94), channel_id=1, source_target_pairs={{0,2},{1,6},{2,3},{3,7},{4,0},{5,4},{6,1},{7,5},{8,10},{9,14},{10,... | collective-permute-start | bytes 786440 | tf_op jit(solution)/shard_map/ppermute | solution.py:185
  17.7 12.4 %collective-permute-start.4 = (bf16[128,1024]{1,0:T(8,128)(2,1)S(1)}, bf16[128,1024]{1,0:T(8,128)(2,1)S(1)}, u32[]{:S(2)}, u32[]{:S(2)}) collective-permute-start(bf16[128,1024]{1,0:T(8,128)(2,1)S(1)} %get-tuple-element.91), channel_id=1, source_target_pairs={{0,3},{1,7},{2,0},{3,4},{4,1},{5,5},{6,2},{7,6},{8,11},{9,15},{10,... | collective-permute-start | bytes 786440 | tf_op jit(solution)/shard_map/ppermute | solution.py:185
  20.2 14.5 %collective-permute-start = (bf16[528,128]{1,0:T(8,128)(2,1)S(1)}, bf16[528,128]{1,0:T(8,128)(2,1)S(1)}, u32[]{:S(2)}, u32[]{:S(2)}) collective-permute-start(bf16[528,128]{1,0:T(8,128)(2,1)S(1)} %fusion.1.key_part), channel_id=1, source_target_pairs={{0,8},{8,16},{16,24},{24,32},{32,40},{40,48},{48,56},{1,9},{9,17},... | collective-permute-start | bytes 405512 | tf_op jit(solution)/shard_map/ppermute | solution.py:210
  23.7 11.6 %collective-permute-start.6 = (bf16[512,128]{1,0:T(8,128)(2,1)S(1)}, bf16[512,128]{1,0:T(8,128)(2,1)S(1)}, u32[]{:S(2)}, u32[]{:S(2)}) collective-permute-start(bf16[512,128]{1,0:T(8,128)(2,1)S(1)} %bitcast.47), channel_id=1, source_target_pairs={{0,8},{8,16},{16,24},{24,32},{32,40},{40,48},{48,56},{1,9},{9,17},... | collective-permute-start | bytes 393224 | tf_op jit(solution)/shard_map/ppermute | solution.py:210
  34.7 2.2 %collective-permute-start.5 = (bf16[528,128]{1,0:T(8,128)(2,1)S(1)}, bf16[528,128]{1,0:T(8,128)(2,1)S(1)}, u32[]{:S(2)}, u32[]{:S(2)}) collective-permute-start(bf16[528,128]{1,0:T(8,128)(2,1)S(1)} %collective-permute-done.key_part), channel_id=1, source_target_pairs={{8,16},{16,24},{24,32},{32,40},{40,48},{48,56},{9,17},{17,25},{25,... | collective-permute-start | bytes 405512 | tf_op jit(solution)/shard_map/ppermute | solution.py:210
  35.4 2.2 %collective-permute-start.8 = (bf16[512,128]{1,0:T(8,128)(2,1)S(1)}, bf16[512,128]{1,0:T(8,128)(2,1)S(1)}, u32[]{:S(2)}, u32[]{:S(2)}) collective-permute-start(bf16[512,128]{1,0:T(8,128)(2,1)S(1)} %collective-permute-done.6.value_part), channel_id=1, source_target_pairs={{8,16},{16,24},{24,32},{32,40},{40,48},{48,56},{9,17},{17,25},{25,... | collective-permute-start | bytes 393224 | tf_op jit(solution)/shard_map/ppermute | solution.py:210
  36.9 2.2 %collective-permute-start.7 = (bf16[528,128]{1,0:T(8,128)(2,1)S(1)}, bf16[528,128]{1,0:T(8,128)(2,1)S(1)}, u32[]{:S(2)}, u32[]{:S(2)}) collective-permute-start(bf16[528,128]{1,0:T(8,128)(2,1)S(1)} %collective-permute-done.5.key_part), channel_id=1, source_target_pairs={{16,24},{24,32},{32,40},{40,48},{48,56},{17,25},{25,33},{33,41},{4... | collective-permute-start | bytes 405512 | tf_op jit(solution)/shard_map/ppermute | solution.py:210
  37.6 2.2 %collective-permute-start.10 = (bf16[512,128]{1,0:T(8,128)(2,1)S(1)}, bf16[512,128]{1,0:T(8,128)(2,1)S(1)}, u32[]{:S(2)}, u32[]{:S(2)}) collective-permute-start(bf16[512,128]{1,0:T(8,128)(2,1)S(1)} %collective-permute-done.8.value_part), channel_id=1, source_target_pairs={{16,24},{24,32},{32,40},{40,48},{48,56},{17,25},{25,33},{33,41},{4... | collective-permute-start | bytes 393224 | tf_op jit(solution)/shard_map/ppermute | solution.py:210
  39.1 2.2 %collective-permute-start.9 = (bf16[528,128]{1,0:T(8,128)(2,1)S(1)}, bf16[528,128]{1,0:T(8,128)(2,1)S(1)}, u32[]{:S(2)}, u32[]{:S(2)}) collective-permute-start(bf16[528,128]{1,0:T(8,128)(2,1)S(1)} %collective-permute-done.7.key_part), channel_id=1, source_target_pairs={{24,32},{32,40},{40,48},{48,56},{25,33},{33,41},{41,49},{49,57},{2... | collective-permute-start | bytes 405512 | tf_op jit(solution)/shard_map/ppermute | solution.py:210
  39.8 2.2 %collective-permute-start.12 = (bf16[512,128]{1,0:T(8,128)(2,1)S(1)}, bf16[512,128]{1,0:T(8,128)(2,1)S(1)}, u32[]{:S(2)}, u32[]{:S(2)}) collective-permute-start(bf16[512,128]{1,0:T(8,128)(2,1)S(1)} %collective-permute-done.10.value_part), channel_id=1, source_target_pairs={{24,32},{32,40},{40,48},{48,56},{25,33},{33,41},{41,49},{49,57},{2... | collective-permute-start | bytes 393224 | tf_op jit(solution)/shard_map/ppermute | solution.py:210
  41.3 2.2 %collective-permute-start.11 = (bf16[528,128]{1,0:T(8,128)(2,1)S(1)}, bf16[528,128]{1,0:T(8,128)(2,1)S(1)}, u32[]{:S(2)}, u32[]{:S(2)}) collective-permute-start(bf16[528,128]{1,0:T(8,128)(2,1)S(1)} %collective-permute-done.9.key_part), channel_id=1, source_target_pairs={{32,40},{40,48},{48,56},{33,41},{41,49},{49,57},{34,42},{42,50},{5... | collective-permute-start | bytes 405512 | tf_op jit(solution)/shard_map/ppermute | solution.py:210
  42.0 2.2 %collective-permute-start.14 = (bf16[512,128]{1,0:T(8,128)(2,1)S(1)}, bf16[512,128]{1,0:T(8,128)(2,1)S(1)}, u32[]{:S(2)}, u32[]{:S(2)}) collective-permute-start(bf16[512,128]{1,0:T(8,128)(2,1)S(1)} %collective-permute-done.12.value_part), channel_id=1, source_target_pairs={{32,40},{40,48},{48,56},{33,41},{41,49},{49,57},{34,42},{42,50},{5... | collective-permute-start | bytes 393224 | tf_op jit(solution)/shard_map/ppermute | solution.py:210
  43.5 47.8 %collective-permute-start.13 = (bf16[528,128]{1,0:T(8,128)(2,1)S(1)}, bf16[528,128]{1,0:T(8,128)(2,1)S(1)}, u32[]{:S(2)}, u32[]{:S(2)}) collective-permute-start(bf16[528,128]{1,0:T(8,128)(2,1)S(1)} %collective-permute-done.11.key_part), channel_id=1, source_target_pairs={{40,48},{48,56},{41,49},{49,57},{42,50},{50,58},{43,51},{51,59},{4... | collective-permute-start | bytes 405512 | tf_op jit(solution)/shard_map/ppermute | solution.py:210
  44.2 47.2 %collective-permute-start.15 = (bf16[512,128]{1,0:T(8,128)(2,1)S(1)}, bf16[512,128]{1,0:T(8,128)(2,1)S(1)}, u32[]{:S(2)}, u32[]{:S(2)}) collective-permute-start(bf16[512,128]{1,0:T(8,128)(2,1)S(1)} %collective-permute-done.14.value_part), channel_id=1, source_target_pairs={{40,48},{48,56},{41,49},{49,57},{42,50},{50,58},{43,51},{51,59},{4... | collective-permute-start | bytes 393224 | tf_op jit(solution)/shard_map/ppermute | solution.py:210
  44.8 0.7 collective-permute-start.16
  45.5 45.8 %collective-permute-start.17 = (bf16[16,128]{1,0:T(8,128)(2,1)S(1)}, bf16[16,128]{1,0:T(8,128)(2,1)S(1)}, u32[]{:S(2)}, u32[]{:S(2)}) collective-permute-start(bf16[16,128]{1,0:T(8,128)(2,1)S(1)} %collective-permute-done.16), channel_id=1, source_target_pairs={{24,8},{16,0},{25,9},{17,1},{26,10},{18,2},{27,11},{19,3},{28,12},... | collective-permute-start | bytes 12296 | tf_op jit(solution)/shard_map/ppermute | solution.py:223
  93.3 63.3 %collective-permute-start.18 = (bf16[128,1024]{1,0:T(8,128)(2,1)S(1)}, bf16[128,1024]{1,0:T(8,128)(2,1)S(1)}, u32[]{:S(2)}, u32[]{:S(2)}) collective-permute-start(bf16[128,1024]{1,0:T(8,128)(2,1)S(1)} %get-tuple-element.87), channel_id=1, source_target_pairs={{0,64},{1,0},{2,68},{3,4},{4,65},{5,1},{6,69},{7,5},{64,128},{65,2... | collective-permute-start | bytes 786440 | tf_op jit(solution)/shard_map/ppermute | solution.py:241
  97.0 67.2 %collective-permute-start.19 = (bf16[128,1024]{1,0:T(8,128)(2,1)S(1)}, bf16[128,1024]{1,0:T(8,128)(2,1)S(1)}, u32[]{:S(2)}, u32[]{:S(2)}) collective-permute-start(bf16[128,1024]{1,0:T(8,128)(2,1)S(1)} %get-tuple-element.90), channel_id=1, source_target_pairs={{0,66},{1,2},{2,70},{3,6},{4,67},{5,3},{6,71},{7,7},{64,130},{65,4... | collective-permute-start | bytes 786440 | tf_op jit(solution)/shard_map/ppermute | solution.py:241
  110.9 60.9 %collective-permute-start.20 = (bf16[128,1024]{1,0:T(8,128)(2,1)S(1)}, bf16[128,1024]{1,0:T(8,128)(2,1)S(1)}, u32[]{:S(2)}, u32[]{:S(2)}) collective-permute-start(bf16[128,1024]{1,0:T(8,128)(2,1)S(1)} %get-tuple-element.89), channel_id=1, source_target_pairs={{0,68},{1,4},{2,64},{3,0},{4,69},{5,5},{6,65},{7,1},{64,132},{65,6... | collective-permute-start | bytes 786440 | tf_op jit(solution)/shard_map/ppermute | solution.py:241
  112.8 76.9 %collective-permute-start.21 = (bf16[128,1024]{1,0:T(8,128)(2,1)S(1)}, bf16[128,1024]{1,0:T(8,128)(2,1)S(1)}, u32[]{:S(2)}, u32[]{:S(2)}) collective-permute-start(bf16[128,1024]{1,0:T(8,128)(2,1)S(1)} %get-tuple-element.88), channel_id=1, source_target_pairs={{0,70},{1,6},{2,66},{3,2},{4,71},{5,7},{6,67},{7,3},{64,134},{65,0... | collective-permute-start | bytes 786440 | tf_op jit(solution)/shard_map/ppermute | solution.py:241
where the time goes:
time: 192 us; the launch traced here: 191 us
  waiting for transfers between devices  112 us (58%)
  starting transfers between devices  63.3 us (33%)
  Pallas kernels  10.5 us (5%)
  other arithmetic  2.89 us (2%)
    ppermute x4, waiting for transfers between devices, local(): received.append(lax.ppermute(out[turn], ('section', 'y', 'core'), route))  66 us
    ppermute x1, waiting for transfers between devices, local(): token = token + lax.ppermute(token, 'row', [(3, 1), (2, 0)])  43.5 us
    ppermute x4, starting transfers between devices, local(): received.append(lax.ppermute(out[turn], ('section', 'y', 'core'), route))  30.3 us
    ppermute x12, starting transfers between devices, hop(): return tuple((lax.ppermute(x, 'row', route) for x in part))  13.8 us
    ppermute x4, starting transfers between devices, local(): blocks.append(lax.ppermute(block[0], ('y', 'core'), route))  12 us
    pallas_call x7, Pallas kernels, attend(): pl.pallas_call(functools.partial(attend_kernel, offset, last), out_shape=...  10.5 us
    all_to_all x1, starting transfers between devices, local(): message = lax.all_to_all(message, ('y', 'core'), 0, 0, tiled=True)  5.14 us
  transfers between devices with their start and end apart: 23, of which 6 were waited for; matrix products, arithmetic and copies ran while one was open for 0% of the time, Pallas kernels for 5%

commit v1 on v0

--- a/solution.py
+++ b/solution.py
@@ -41,11 +41,14 @@
     rate = math.log2(math.e) / math.sqrt(HD)
     docs = query_docs[0:1, :]
 
-    def fold(masked):
+    key_docs = key_part[span : span + YS, :].astype(jnp.float32)
+
+    def fold(single):
         keys = key_part[:span, :]
         values = value_part[...]
-        if masked:
-            key_docs = key_part[span : span + YS, :].astype(jnp.float32)
+        if single:
+            whole = docs == jnp.max(key_docs)
+        else:
             start = jnp.zeros((1, span), jnp.float32)
             for doc in range(1, 4):
                 below = jnp.sum((key_docs < doc).astype(jnp.float32))
@@ -62,7 +65,7 @@
             )
 
         def one_head(head, scores):
-            if masked:
+            if not single:
                 key_pos = lax.broadcasted_iota(jnp.int32, (span, span), 0)
                 allowed = key_pos >= start
                 if offset == 0:
@@ -73,7 +76,11 @@
             if offset:
                 old_max = old_max_ref[pl.ds(head, 1), :]
                 top = jnp.maximum(old_max, top)
-            terms = jnp.exp2((scores - top) * rate)
+            shift = top
+            if single:
+                top = jnp.where(whole, top, old_max)
+                shift = jnp.where(whole, top, -MASKED)
+            terms = jnp.exp2((scores - shift) * rate)
             total = jnp.sum(terms, axis=0, keepdims=True)
             product = lax.dot_general(
                 values,
@@ -100,15 +107,13 @@
         lax.fori_loop(0, heads // 2, two_heads, 0)
 
     if offset == 0:
-        fold(True)
+        fold(False)
     else:
-        key_docs = key_part[span : span + YS, :].astype(jnp.float32)
         low = jnp.min(key_docs)
-        first_doc = jnp.min(docs)
-        last_doc = jnp.max(docs)
-        live = (place[0] >= offset) & (jnp.max(key_docs) >= first_doc)
-        pl.when(live & (low >= last_doc))(functools.partial(fold, False))
-        pl.when(live & (low < last_doc))(functools.partial(fold, True))
+        high = jnp.max(key_docs)
+        live = (place[0] >= offset) & (high >= jnp.min(docs))
+        pl.when(live & (low == high))(functools.partial(fold, True))
+        pl.when(live & (low < high))(functools.partial(fold, False))
 
         @pl.when(jnp.logical_not(live))
         def _():
@@ -219,8 +224,7 @@
             part = (keys, part[1])
             later = hop(part, step + 1)
         if step == BACK - 1:
-            token = lax.ppermute(part[0][YS * HD :], "row", [(7, 3), (6, 2), (5, 4)])
-            token = token + lax.ppermute(token, "row", [(3, 1), (2, 0)])
+            token = lax.ppermute(part[0][YS * HD :], "row", [(7, 3), (6, 2)])
         held = [own, *state] + ([token] if step == BACK else [])
         state = attend(place, query_docs, part, step, held, step == BACK)
         part = later

time: 192 us -> 185 us (0.964)
  the two profiles are of different devices: /device:TPU:3 before, /device:TPU:84 now
where the time goes in v1:
time: 185 us; the launch traced here: 182 us
  waiting for transfers between devices  90.6 us (49%)
  starting transfers between devices  71.6 us (39%)
  Pallas kernels  15.2 us (8%)
  other arithmetic  2.88 us (2%)
    ppermute x4, waiting for transfers between devices, local(): received.append(lax.ppermute(out[turn], ('section', 'y', 'core'), route))  49.6 us
    ppermute x1, waiting for transfers between devices, local(): token = lax.ppermute(part[0][YS * HD:], 'row', [(7, 3), (6, 2)])  39.9 us
    ppermute x4, starting transfers between devices, local(): received.append(lax.ppermute(out[turn], ('section', 'y', 'core'), route))  28.7 us
    ppermute x12, starting transfers between devices, hop(): return tuple((lax.ppermute(x, 'row', route) for x in part))  25 us
    pallas_call x7, Pallas kernels, attend(): pl.pallas_call(functools.partial(attend_kernel, offset, last), out_shape=...  15.2 us
    ppermute x4, starting transfers between devices, local(): blocks.append(lax.ppermute(block[0], ('y', 'core'), route))  11.8 us
    all_to_all x1, starting transfers between devices, local(): message = lax.all_to_all(message, ('y', 'core'), 0, 0, tiled=True)  4.8 us
  transfers between devices with their start and end apart: 22, of which 5 were waited for; matrix products, arithmetic and copies ran while one was open for 0% of the time, Pallas kernels for 7%

profile of v1, /device:TPU:84, one launch (start us, length us, event | category | flops | bytes accessed | tf_op | source)
XLA Modules:
  0.0 182.3 jit_solution(3359003480571897)
XLA Ops:
  0.0 0.8 convert_element_type.19
  0.8 1.0 reshape_squeeze.6
  1.9 0.7 pad_maximum_fusion.1
  2.7 4.8 %all-to-all-start = ((bf16[8,144,128]{2,1,0:T(8,128)(2,1)}), bf16[8,144,128]{2,1,0:T(8,128)(2,1)S(1)}, u32[]{:S(2)}, u32[]{:S(2)}) async-start(bf16[8,144,128]{2,1,0:T(8,128)(2,1)} %pad_maximum_fusion.1), calls=%async_computation | async-start | bytes 589824 | tf_op jit(solution)/shard_map/all_to_all | solution.py:199
  7.6 2.5 %collective-permute-start.1 = (bf16[128,1024]{1,0:T(8,128)(2,1)S(1)}, bf16[128,1024]{1,0:T(8,128)(2,1)S(1)}, u32[]{:S(2)}, u32[]{:S(2)}) collective-permute-start(bf16[128,1024]{1,0:T(8,128)(2,1)S(1)} %get-tuple-element.93), channel_id=1, source_target_pairs={{0,0},{1,4},{2,1},{3,5},{4,2},{5,6},{6,3},{7,7},{8,8},{9,12},{10,9... | collective-permute-start | bytes 786440 | tf_op jit(solution)/shard_map/ppermute | solution.py:190
  10.1 2.8 %collective-permute-start.2 = (bf16[128,1024]{1,0:T(8,128)(2,1)S(1)}, bf16[128,1024]{1,0:T(8,128)(2,1)S(1)}, u32[]{:S(2)}, u32[]{:S(2)}) collective-permute-start(bf16[128,1024]{1,0:T(8,128)(2,1)S(1)} %get-tuple-element.92), channel_id=1, source_target_pairs={{0,1},{1,5},{2,2},{3,6},{4,3},{5,7},{6,0},{7,4},{8,9},{9,13},{10,1... | collective-permute-start | bytes 786440 | tf_op jit(solution)/shard_map/ppermute | solution.py:190
  12.9 4.1 %collective-permute-start.3 = (bf16[128,1024]{1,0:T(8,128)(2,1)S(1)}, bf16[128,1024]{1,0:T(8,128)(2,1)S(1)}, u32[]{:S(2)}, u32[]{:S(2)}) collective-permute-start(bf16[128,1024]{1,0:T(8,128)(2,1)S(1)} %get-tuple-element.94), channel_id=1, source_target_pairs={{0,2},{1,6},{2,3},{3,7},{4,0},{5,4},{6,1},{7,5},{8,10},{9,14},{10,... | collective-permute-start | bytes 786440 | tf_op jit(solution)/shard_map/ppermute | solution.py:190
  17.0 2.4 %collective-permute-start.4 = (bf16[128,1024]{1,0:T(8,128)(2,1)S(1)}, bf16[128,1024]{1,0:T(8,128)(2,1)S(1)}, u32[]{:S(2)}, u32[]{:S(2)}) collective-permute-start(bf16[128,1024]{1,0:T(8,128)(2,1)S(1)} %get-tuple-element.91), channel_id=1, source_target_pairs={{0,3},{1,7},{2,0},{3,4},{4,1},{5,5},{6,2},{7,6},{8,11},{9,15},{10,... | collective-permute-start | bytes 786440 | tf_op jit(solution)/shard_map/ppermute | solution.py:190
  19.7 3.8 %collective-permute-start = (bf16[528,128]{1,0:T(8,128)(2,1)S(1)}, bf16[528,128]{1,0:T(8,128)(2,1)S(1)}, u32[]{:S(2)}, u32[]{:S(2)}) collective-permute-start(bf16[528,128]{1,0:T(8,128)(2,1)S(1)} %fusion.1.key_part), channel_id=1, source_target_pairs={{0,8},{8,16},{16,24},{24,32},{32,40},{40,48},{48,56},{1,9},{9,17},... | collective-permute-start | bytes 405512 | tf_op jit(solution)/shard_map/ppermute | solution.py:215
  23.5 5.0 %collective-permute-start.6 = (bf16[512,128]{1,0:T(8,128)(2,1)S(1)}, bf16[512,128]{1,0:T(8,128)(2,1)S(1)}, u32[]{:S(2)}, u32[]{:S(2)}) collective-permute-start(bf16[512,128]{1,0:T(8,128)(2,1)S(1)} %bitcast.47), channel_id=1, source_target_pairs={{0,8},{8,16},{16,24},{24,32},{32,40},{40,48},{48,56},{1,9},{9,17},... | collective-permute-start | bytes 393224 | tf_op jit(solution)/shard_map/ppermute | solution.py:215
  28.7 4.6 %attend.7 = (bf16[512,1024]{1,0:T(8,128)(2,1)S(1)}, f32[8,512]{1,0:T(8,128)S(1)}, f32[8,512]{1,0:T(8,128)S(1)}, f32[8,128,512]{2,1,0:T(8,128)S(1)}) custom-call(s32[3]{0:T(128)S(1)} %pad_add_fusion.place, f32[8,512]{1,0:T(8,128)S(1)} %broadcast_in_dim.21.query_docs, bf16[528,128]{1,0:T(8,128)(2,1)S(1)} %fusion.1.key_part, bf16[512,128]{1,0:T(8,128)(2,1)S(1)} %bitcast.48, ...), custom_call_target="tpu_custom_call" | custom-call | flops 1073741824 | bytes 5242880 | tf_op jit(solution)/shard_map/attend/pallas_call | solution.py:156
  33.3 3.8 %collective-permute-start.5 = (bf16[528,128]{1,0:T(8,128)(2,1)S(1)}, bf16[528,128]{1,0:T(8,128)(2,1)S(1)}, u32[]{:S(2)}, u32[]{:S(2)}) collective-permute-start(bf16[528,128]{1,0:T(8,128)(2,1)S(1)} %collective-permute-done.key_part), channel_id=1, source_target_pairs={{8,16},{16,24},{24,32},{32,40},{40,48},{48,56},{9,17},{17,25},{25,... | collective-permute-start | bytes 405512 | tf_op jit(solution)/shard_map/ppermute | solution.py:215
  37.1 3.8 %collective-permute-start.8 = (bf16[512,128]{1,0:T(8,128)(2,1)S(1)}, bf16[512,128]{1,0:T(8,128)(2,1)S(1)}, u32[]{:S(2)}, u32[]{:S(2)}) collective-permute-start(bf16[512,128]{1,0:T(8,128)(2,1)S(1)} %collective-permute-done.6.value_part), channel_id=1, source_target_pairs={{8,16},{16,24},{24,32},{32,40},{40,48},{48,56},{9,17},{17,25},{25,... | collective-permute-start | bytes 393224 | tf_op jit(solution)/shard_map/ppermute | solution.py:215
  41.0 5.3 %attend.8 = (f32[8,512]{1,0:T(8,128)S(1)}, f32[8,512]{1,0:T(8,128)S(1)}, f32[8,128,512]{2,1,0:T(8,128)S(1)}) custom-call(s32[3]{0:T(128)S(1)} %pad_add_fusion.place, f32[8,512]{1,0:T(8,128)S(1)} %broadcast_in_dim.21.query_docs, bf16[528,128]{1,0:T(8,128)(2,1)S(1)} %collective-permute-done.key_part, bf16[512,128]{1,0:T(8,128)(2,1)S(1)} %collective-permute-done.6.value_part, ...), custom_call_target="tpu_custom_call" | custom-call | flops 1073741824 | bytes 5242880 | tf_op jit(solution)/shard_map/attend/pallas_call | solution.py:156
  46.3 2.5 %collective-permute-start.7 = (bf16[528,128]{1,0:T(8,128)(2,1)S(1)}, bf16[528,128]{1,0:T(8,128)(2,1)S(1)}, u32[]{:S(2)}, u32[]{:S(2)}) collective-permute-start(bf16[528,128]{1,0:T(8,128)(2,1)S(1)} %collective-permute-done.5.key_part), channel_id=1, source_target_pairs={{16,24},{24,32},{32,40},{40,48},{48,56},{17,25},{25,33},{33,41},{4... | collective-permute-start | bytes 405512 | tf_op jit(solution)/shard_map/ppermute | solution.py:215
  48.8 1.9 %collective-permute-start.10 = (bf16[512,128]{1,0:T(8,128)(2,1)S(1)}, bf16[512,128]{1,0:T(8,128)(2,1)S(1)}, u32[]{:S(2)}, u32[]{:S(2)}) collective-permute-start(bf16[512,128]{1,0:T(8,128)(2,1)S(1)} %collective-permute-done.8.value_part), channel_id=1, source_target_pairs={{16,24},{24,32},{32,40},{40,48},{48,56},{17,25},{25,33},{33,41},{4... | collective-permute-start | bytes 393224 | tf_op jit(solution)/shard_map/ppermute | solution.py:215
  50.8 0.8 attend.9
  52.3 1.0 collective-permute-done.10.value_part
  53.9 0.8 attend.10
  56.1 0.8 attend.11
  58.3 1.3 collective-permute-start.16
  59.6 1.0 attend.12
  60.6 39.9 %collective-permute-done.16.refs_4_ = bf16[16,128]{1,0:T(8,128)(2,1)S(1)} collective-permute-done((bf16[16,128]{1,0:T(8,128)(2,1)S(1)}, bf16[16,128]{1,0:T(8,128)(2,1)S(1)}, u32[]{:S(2)}, u32[]{:S(2)}) %collective-permute-start.16) | collective-permute-done | bytes 4128 | tf_op jit(solution)/shard_map/ppermute | solution.py:227
  100.6 1.9 %attend.13 = bf16[4,128,1024]{2,1,0:T(8,128)(2,1)S(1)} custom-call(s32[3]{0:T(128)S(1)} %pad_add_fusion.place, f32[8,512]{1,0:T(8,128)S(1)} %broadcast_in_dim.21.query_docs, bf16[528,128]{1,0:T(8,128)(2,1)S(1)} %collective-permute-done.13.key_part, bf16[512,128]{1,0:T(8,128)(2,1)S(1)} %collective-permute-done.15.value_part, ...), custom_call_target="tpu_custom_call" | custom-call | flops 1073741824 | bytes 5242880 | tf_op jit(solution)/shard_map/attend/pallas_call | solution.py:156
  102.5 3.3 %collective-permute-start.17 = (bf16[128,1024]{1,0:T(8,128)(2,1)S(1)}, bf16[128,1024]{1,0:T(8,128)(2,1)S(1)}, u32[]{:S(2)}, u32[]{:S(2)}) collective-permute-start(bf16[128,1024]{1,0:T(8,128)(2,1)S(1)} %get-tuple-element.87), channel_id=1, source_target_pairs={{0,64},{1,0},{2,68},{3,4},{4,65},{5,1},{6,69},{7,5},{64,128},{65,2... | collective-permute-start | bytes 786440 | tf_op jit(solution)/shard_map/ppermute | solution.py:245
  105.8 15.2 %collective-permute-start.18 = (bf16[128,1024]{1,0:T(8,128)(2,1)S(1)}, bf16[128,1024]{1,0:T(8,128)(2,1)S(1)}, u32[]{:S(2)}, u32[]{:S(2)}) collective-permute-start(bf16[128,1024]{1,0:T(8,128)(2,1)S(1)} %get-tuple-element.90), channel_id=1, source_target_pairs={{0,66},{1,2},{2,70},{3,6},{4,67},{5,3},{6,71},{7,7},{64,130},{65,4... | collective-permute-start | bytes 786440 | tf_op jit(solution)/shard_map/ppermute | solution.py:245
  121.0 1.9 %collective-permute-start.19 = (bf16[128,1024]{1,0:T(8,128)(2,1)S(1)}, bf16[128,1024]{1,0:T(8,128)(2,1)S(1)}, u32[]{:S(2)}, u32[]{:S(2)}) collective-permute-start(bf16[128,1024]{1,0:T(8,128)(2,1)S(1)} %get-tuple-element.89), channel_id=1, source_target_pairs={{0,68},{1,4},{2,64},{3,0},{4,69},{5,5},{6,65},{7,1},{64,132},{65,6... | collective-permute-start | bytes 786440 | tf_op jit(solution)/shard_map/ppermute | solution.py:245
  122.9 8.3 %collective-permute-start.20 = (bf16[128,1024]{1,0:T(8,128)(2,1)S(1)}, bf16[128,1024]{1,0:T(8,128)(2,1)S(1)}, u32[]{:S(2)}, u32[]{:S(2)}) collective-permute-start(bf16[128,1024]{1,0:T(8,128)(2,1)S(1)} %get-tuple-element.88), channel_id=1, source_target_pairs={{0,70},{1,6},{2,66},{3,2},{4,71},{5,7},{6,67},{7,3},{64,134},{65,0... | collective-permute-start | bytes 786440 | tf_op jit(solution)/shard_map/ppermute | solution.py:245
  131.3 9.9 %collective-permute-done.17 = bf16[128,1024]{1,0:T(8,128)(2,1)S(1)} collective-permute-done((bf16[128,1024]{1,0:T(8,128)(2,1)S(1)}, bf16[128,1024]{1,0:T(8,128)(2,1)S(1)}, u32[]{:S(2)}, u32[]{:S(2)}) %collective-permute-start.17) | collective-permute-done | bytes 262176 | tf_op jit(solution)/shard_map/ppermute | solution.py:245
  141.3 18.6 %collective-permute-done.19 = bf16[128,1024]{1,0:T(8,128)(2,1)S(1)} collective-permute-done((bf16[128,1024]{1,0:T(8,128)(2,1)S(1)}, bf16[128,1024]{1,0:T(8,128)(2,1)S(1)}, u32[]{:S(2)}, u32[]{:S(2)}) %collective-permute-start.19) | collective-permute-done | bytes 262176 | tf_op jit(solution)/shard_map/ppermute | solution.py:245
  159.9 21.0 %collective-permute-done.20 = bf16[128,1024]{1,0:T(8,128)(2,1)S(1)} collective-permute-done((bf16[128,1024]{1,0:T(8,128)(2,1)S(1)}, bf16[128,1024]{1,0:T(8,128)(2,1)S(1)}, u32[]{:S(2)}, u32[]{:S(2)}) %collective-permute-start.20) | collective-permute-done | bytes 262176 | tf_op jit(solution)/shard_map/ppermute | solution.py:245
  181.3 1.1 maximum_bitcast_fusion
  (44 shorter events, 5.0 us)
Async XLA Ops:
  0.0 7.5 %copy-start = (bf16[1,2,128,2048]{3,2,1,0:T(8,128)(2,1)S(1)}, bf16[1,2,128,2048]{3,2,1,0:T(8,128)(2,1)}, u32[]{:S(2)}) copy-start(bf16[1,2,128,2048]{3,2,1,0:T(8,128)(2,1)} %param.3) | copy-start | bytes 3145732
  2.7 16.9 %all-to-all-start = ((bf16[8,144,128]{2,1,0:T(8,128)(2,1)}), bf16[8,144,128]{2,1,0:T(8,128)(2,1)S(1)}, u32[]{:S(2)}, u32[]{:S(2)}) async-start(bf16[8,144,128]{2,1,0:T(8,128)(2,1)} %pad_maximum_fusion.1), calls=%async_computation | async-start | bytes 589824 | tf_op jit(solution)/shard_map/all_to_all | solution.py:199
  7.6 16.0 %collective-permute-start.1 = (bf16[128,1024]{1,0:T(8,128)(2,1)S(1)}, bf16[128,1024]{1,0:T(8,128)(2,1)S(1)}, u32[]{:S(2)}, u32[]{:S(2)}) collective-permute-start(bf16[128,1024]{1,0:T(8,128)(2,1)S(1)} %get-tuple-element.93), channel_id=1, source_target_pairs={{0,0},{1,4},{2,1},{3,5},{4,2},{5,6},{6,3},{7,7},{8,8},{9,12},{10,9... | collective-permute-start | bytes 786440 | tf_op jit(solution)/shard_map/ppermute | solution.py:190
  10.1 18.6 %collective-permute-start.2 = (bf16[128,1024]{1,0:T(8,128)(2,1)S(1)}, bf16[128,1024]{1,0:T(8,128)(2,1)S(1)}, u32[]{:S(2)}, u32[]{:S(2)}) collective-permute-start(bf16[128,1024]{1,0:T(8,128)(2,1)S(1)} %get-tuple-element.92), channel_id=1, source_target_pairs={{0,1},{1,5},{2,2},{3,6},{4,3},{5,7},{6,0},{7,4},{8,9},{9,13},{10,1... | collective-permute-start | bytes 786440 | tf_op jit(solution)/shard_map/ppermute | solution.py:190
  12.9 15.8 %collective-permute-start.3 = (bf16[128,1024]{1,0:T(8,128)(2,1)S(1)}, bf16[128,1024]{1,0:T(8,128)(2,1)S(1)}, u32[]{:S(2)}, u32[]{:S(2)}) collective-permute-start(bf16[128,1024]{1,0:T(8,128)(2,1)S(1)} %get-tuple-element.94), channel_id=1, source_target_pairs={{0,2},{1,6},{2,3},{3,7},{4,0},{5,4},{6,1},{7,5},{8,10},{9,14},{10,... | collective-permute-start | bytes 786440 | tf_op jit(solution)/shard_map/ppermute | solution.py:190
  17.0 11.7 %collective-permute-start.4 = (bf16[128,1024]{1,0:T(8,128)(2,1)S(1)}, bf16[128,1024]{1,0:T(8,128)(2,1)S(1)}, u32[]{:S(2)}, u32[]{:S(2)}) collective-permute-start(bf16[128,1024]{1,0:T(8,128)(2,1)S(1)} %get-tuple-element.91), channel_id=1, source_target_pairs={{0,3},{1,7},{2,0},{3,4},{4,1},{5,5},{6,2},{7,6},{8,11},{9,15},{10,... | collective-permute-start | bytes 786440 | tf_op jit(solution)/shard_map/ppermute | solution.py:190
  19.7 13.6 %collective-permute-start = (bf16[528,128]{1,0:T(8,128)(2,1)S(1)}, bf16[528,128]{1,0:T(8,128)(2,1)S(1)}, u32[]{:S(2)}, u32[]{:S(2)}) collective-permute-start(bf16[528,128]{1,0:T(8,128)(2,1)S(1)} %fusion.1.key_part), channel_id=1, source_target_pairs={{0,8},{8,16},{16,24},{24,32},{32,40},{40,48},{48,56},{1,9},{9,17},... | collective-permute-start | bytes 405512 | tf_op jit(solution)/shard_map/ppermute | solution.py:215
  23.5 13.6 %collective-permute-start.6 = (bf16[512,128]{1,0:T(8,128)(2,1)S(1)}, bf16[512,128]{1,0:T(8,128)(2,1)S(1)}, u32[]{:S(2)}, u32[]{:S(2)}) collective-permute-start(bf16[512,128]{1,0:T(8,128)(2,1)S(1)} %bitcast.47), channel_id=1, source_target_pairs={{0,8},{8,16},{16,24},{24,32},{32,40},{40,48},{48,56},{1,9},{9,17},... | collective-permute-start | bytes 393224 | tf_op jit(solution)/shard_map/ppermute | solution.py:215
  33.3 13.0 %collective-permute-start.5 = (bf16[528,128]{1,0:T(8,128)(2,1)S(1)}, bf16[528,128]{1,0:T(8,128)(2,1)S(1)}, u32[]{:S(2)}, u32[]{:S(2)}) collective-permute-start(bf16[528,128]{1,0:T(8,128)(2,1)S(1)} %collective-permute-done.key_part), channel_id=1, source_target_pairs={{8,16},{16,24},{24,32},{32,40},{40,48},{48,56},{9,17},{17,25},{25,... | collective-permute-start | bytes 405512 | tf_op jit(solution)/shard_map/ppermute | solution.py:215
  37.1 11.7 %collective-permute-start.8 = (bf16[512,128]{1,0:T(8,128)(2,1)S(1)}, bf16[512,128]{1,0:T(8,128)(2,1)S(1)}, u32[]{:S(2)}, u32[]{:S(2)}) collective-permute-start(bf16[512,128]{1,0:T(8,128)(2,1)S(1)} %collective-permute-done.6.value_part), channel_id=1, source_target_pairs={{8,16},{16,24},{24,32},{32,40},{40,48},{48,56},{9,17},{17,25},{25,... | collective-permute-start | bytes 393224 | tf_op jit(solution)/shard_map/ppermute | solution.py:215
  46.3 5.3 %collective-permute-start.7 = (bf16[528,128]{1,0:T(8,128)(2,1)S(1)}, bf16[528,128]{1,0:T(8,128)(2,1)S(1)}, u32[]{:S(2)}, u32[]{:S(2)}) collective-permute-start(bf16[528,128]{1,0:T(8,128)(2,1)S(1)} %collective-permute-done.5.key_part), channel_id=1, source_target_pairs={{16,24},{24,32},{32,40},{40,48},{48,56},{17,25},{25,33},{33,41},{4... | collective-permute-start | bytes 405512 | tf_op jit(solution)/shard_map/ppermute | solution.py:215
  48.8 4.4 %collective-permute-start.10 = (bf16[512,128]{1,0:T(8,128)(2,1)S(1)}, bf16[512,128]{1,0:T(8,128)(2,1)S(1)}, u32[]{:S(2)}, u32[]{:S(2)}) collective-permute-start(bf16[512,128]{1,0:T(8,128)(2,1)S(1)} %collective-permute-done.8.value_part), channel_id=1, source_target_pairs={{16,24},{24,32},{32,40},{40,48},{48,56},{17,25},{25,33},{33,41},{4... | collective-permute-start | bytes 393224 | tf_op jit(solution)/shard_map/ppermute | solution.py:215
  51.6 3.2 %collective-permute-start.9 = (bf16[528,128]{1,0:T(8,128)(2,1)S(1)}, bf16[528,128]{1,0:T(8,128)(2,1)S(1)}, u32[]{:S(2)}, u32[]{:S(2)}) collective-permute-start(bf16[528,128]{1,0:T(8,128)(2,1)S(1)} %collective-permute-done.7.key_part), channel_id=1, source_target_pairs={{24,32},{32,40},{40,48},{48,56},{25,33},{33,41},{41,49},{49,57},{2... | collective-permute-start | bytes 405512 | tf_op jit(solution)/shard_map/ppermute | solution.py:215
  53.3 2.2 %collective-permute-start.12 = (bf16[512,128]{1,0:T(8,128)(2,1)S(1)}, bf16[512,128]{1,0:T(8,128)(2,1)S(1)}, u32[]{:S(2)}, u32[]{:S(2)}) collective-permute-start(bf16[512,128]{1,0:T(8,128)(2,1)S(1)} %collective-permute-done.10.value_part), channel_id=1, source_target_pairs={{24,32},{32,40},{40,48},{48,56},{25,33},{33,41},{41,49},{49,57},{2... | collective-permute-start | bytes 393224 | tf_op jit(solution)/shard_map/ppermute | solution.py:215
  54.8 2.2 %collective-permute-start.11 = (bf16[528,128]{1,0:T(8,128)(2,1)S(1)}, bf16[528,128]{1,0:T(8,128)(2,1)S(1)}, u32[]{:S(2)}, u32[]{:S(2)}) collective-permute-start(bf16[528,128]{1,0:T(8,128)(2,1)S(1)} %collective-permute-done.9.key_part), channel_id=1, source_target_pairs={{32,40},{40,48},{48,56},{33,41},{41,49},{49,57},{34,42},{42,50},{5... | collective-permute-start | bytes 405512 | tf_op jit(solution)/shard_map/ppermute | solution.py:215
  55.5 2.2 %collective-permute-start.14 = (bf16[512,128]{1,0:T(8,128)(2,1)S(1)}, bf16[512,128]{1,0:T(8,128)(2,1)S(1)}, u32[]{:S(2)}, u32[]{:S(2)}) collective-permute-start(bf16[512,128]{1,0:T(8,128)(2,1)S(1)} %collective-permute-done.12.value_part), channel_id=1, source_target_pairs={{32,40},{40,48},{48,56},{33,41},{41,49},{49,57},{34,42},{42,50},{5... | collective-permute-start | bytes 393224 | tf_op jit(solution)/shard_map/ppermute | solution.py:215
  57.0 43.6 %collective-permute-start.13 = (bf16[528,128]{1,0:T(8,128)(2,1)S(1)}, bf16[528,128]{1,0:T(8,128)(2,1)S(1)}, u32[]{:S(2)}, u32[]{:S(2)}) collective-permute-start(bf16[528,128]{1,0:T(8,128)(2,1)S(1)} %collective-permute-done.11.key_part), channel_id=1, source_target_pairs={{40,48},{48,56},{41,49},{49,57},{42,50},{50,58},{43,51},{51,59},{4... | collective-permute-start | bytes 405512 | tf_op jit(solution)/shard_map/ppermute | solution.py:215
  57.7 42.9 %collective-permute-start.15 = (bf16[512,128]{1,0:T(8,128)(2,1)S(1)}, bf16[512,128]{1,0:T(8,128)(2,1)S(1)}, u32[]{:S(2)}, u32[]{:S(2)}) collective-permute-start(bf16[512,128]{1,0:T(8,128)(2,1)S(1)} %collective-permute-done.14.value_part), channel_id=1, source_target_pairs={{40,48},{48,56},{41,49},{49,57},{42,50},{50,58},{43,51},{51,59},{4... | collective-permute-start | bytes 393224 | tf_op jit(solution)/shard_map/ppermute | solution.py:215
  58.3 42.2 %collective-permute-start.16 = (bf16[16,128]{1,0:T(8,128)(2,1)S(1)}, bf16[16,128]{1,0:T(8,128)(2,1)S(1)}, u32[]{:S(2)}, u32[]{:S(2)}) collective-permute-start(bf16[16,128]{1,0:T(8,128)(2,1)S(1)} %slice.27), channel_id=1, source_target_pairs={{56,24},{48,16},{57,25},{49,17},{58,26},{50,18},{59,27},{51,19},{6... | collective-permute-start | bytes 12296 | tf_op jit(solution)/shard_map/ppermute | solution.py:227
  102.5 38.7 %collective-permute-start.17 = (bf16[128,1024]{1,0:T(8,128)(2,1)S(1)}, bf16[128,1024]{1,0:T(8,128)(2,1)S(1)}, u32[]{:S(2)}, u32[]{:S(2)}) collective-permute-start(bf16[128,1024]{1,0:T(8,128)(2,1)S(1)} %get-tuple-element.87), channel_id=1, source_target_pairs={{0,64},{1,0},{2,68},{3,4},{4,65},{5,1},{6,69},{7,5},{64,128},{65,2... | collective-permute-start | bytes 786440 | tf_op jit(solution)/shard_map/ppermute | solution.py:245
  105.8 35.5 %collective-permute-start.18 = (bf16[128,1024]{1,0:T(8,128)(2,1)S(1)}, bf16[128,1024]{1,0:T(8,128)(2,1)S(1)}, u32[]{:S(2)}, u32[]{:S(2)}) collective-permute-start(bf16[128,1024]{1,0:T(8,128)(2,1)S(1)} %get-tuple-element.90), channel_id=1, source_target_pairs={{0,66},{1,2},{2,70},{3,6},{4,67},{5,3},{6,71},{7,7},{64,130},{65,4... | collective-permute-start | bytes 786440 | tf_op jit(solution)/shard_map/ppermute | solution.py:245
  121.0 38.9 %collective-permute-start.19 = (bf16[128,1024]{1,0:T(8,128)(2,1)S(1)}, bf16[128,1024]{1,0:T(8,128)(2,1)S(1)}, u32[]{:S(2)}, u32[]{:S(2)}) collective-permute-start(bf16[128,1024]{1,0:T(8,128)(2,1)S(1)} %get-tuple-element.89), channel_id=1, source_target_pairs={{0,68},{1,4},{2,64},{3,0},{4,69},{5,5},{6,65},{7,1},{64,132},{65,6... | collective-permute-start | bytes 786440 | tf_op jit(solution)/shard_map/ppermute | solution.py:245
  122.9 58.0 %collective-permute-start.20 = (bf16[128,1024]{1,0:T(8,128)(2,1)S(1)}, bf16[128,1024]{1,0:T(8,128)(2,1)S(1)}, u32[]{:S(2)}, u32[]{:S(2)}) collective-permute-start(bf16[128,1024]{1,0:T(8,128)(2,1)S(1)} %get-tuple-element.88), channel_id=1, source_target_pairs={{0,70},{1,6},{2,66},{3,2},{4,71},{5,7},{6,67},{7,3},{64,134},{65,0... | collective-permute-start | bytes 786440 | tf_op jit(solution)/shard_map/ppermute | solution.py:245

commit v2 on v1

--- a/solution.py
+++ b/solution.py
@@ -223,8 +223,8 @@
             keys, state = lax.optimization_barrier((part[0], state))
             part = (keys, part[1])
             later = hop(part, step + 1)
-        if step == BACK - 1:
-            token = lax.ppermute(part[0][YS * HD :], "row", [(7, 3), (6, 2)])
+        if step == BACK - 2:
+            token = lax.ppermute(part[0][YS * HD :], "row", [(7, 3), (6, 2), (5, 4)])
         held = [own, *state] + ([token] if step == BACK else [])
         state = attend(place, query_docs, part, step, held, step == BACK)
         part = later

time: 185 us -> 185 us (level)
  the two profiles are of different devices: /device:TPU:84 before, /device:TPU:94 now
where the time goes in v2:
time: 185 us; the launch traced here: 184 us
  waiting for transfers between devices  99.9 us (54%)
  starting transfers between devices  68.9 us (37%)
  Pallas kernels  10.7 us (6%)
  other arithmetic  2.88 us (2%)
    ppermute x4, waiting for transfers between devices, local(): received.append(lax.ppermute(out[turn], ('section', 'y', 'core'), route))  57.4 us
    ppermute x1, waiting for transfers between devices, local(): token = lax.ppermute(part[0][YS * HD:], 'row', [(7, 3), (6, 2), (5, 4)])  40.5 us
    ppermute x12, starting transfers between devices, hop(): return tuple((lax.ppermute(x, 'row', route) for x in part))  29.9 us
    ppermute x4, starting transfers between devices, local(): received.append(lax.ppermute(out[turn], ('section', 'y', 'core'), route))  20.5 us
    ppermute x4, starting transfers between devices, local(): blocks.append(lax.ppermute(block[0], ('y', 'core'), route))  12.5 us
    pallas_call x7, Pallas kernels, attend(): pl.pallas_call(functools.partial(attend_kernel, offset, last), out_shape=...  10.7 us
    all_to_all x1, starting transfers between devices, local(): message = lax.all_to_all(message, ('y', 'core'), 0, 0, tiled=True)  4.69 us
  transfers between devices with their start and end apart: 22, of which 5 were waited for; matrix products, arithmetic and copies ran while one was open for 0% of the time, Pallas kernels for 5%

profile of v2, /device:TPU:94, one launch (start us, length us, event | category | flops | bytes accessed | tf_op | source)
XLA Modules:
  0.0 184.5 jit_solution(7972975965964183939)
XLA Ops:
  0.0 0.8 convert_element_type.19
  0.8 1.0 reshape_squeeze.6
  1.9 0.7 pad_maximum_fusion.1
  2.7 4.7 %all-to-all-start = ((bf16[8,144,128]{2,1,0:T(8,128)(2,1)}), bf16[8,144,128]{2,1,0:T(8,128)(2,1)S(1)}, u32[]{:S(2)}, u32[]{:S(2)}) async-start(bf16[8,144,128]{2,1,0:T(8,128)(2,1)} %pad_maximum_fusion.1), calls=%async_computation | async-start | bytes 589824 | tf_op jit(solution)/shard_map/all_to_all | solution.py:199
  7.5 3.1 %collective-permute-start.1 = (bf16[128,1024]{1,0:T(8,128)(2,1)S(1)}, bf16[128,1024]{1,0:T(8,128)(2,1)S(1)}, u32[]{:S(2)}, u32[]{:S(2)}) collective-permute-start(bf16[128,1024]{1,0:T(8,128)(2,1)S(1)} %get-tuple-element.93), channel_id=1, source_target_pairs={{0,0},{1,4},{2,1},{3,5},{4,2},{5,6},{6,3},{7,7},{8,8},{9,12},{10,9... | collective-permute-start | bytes 786440 | tf_op jit(solution)/shard_map/ppermute | solution.py:190
  10.6 1.9 %collective-permute-start.2 = (bf16[128,1024]{1,0:T(8,128)(2,1)S(1)}, bf16[128,1024]{1,0:T(8,128)(2,1)S(1)}, u32[]{:S(2)}, u32[]{:S(2)}) collective-permute-start(bf16[128,1024]{1,0:T(8,128)(2,1)S(1)} %get-tuple-element.92), channel_id=1, source_target_pairs={{0,1},{1,5},{2,2},{3,6},{4,3},{5,7},{6,0},{7,4},{8,9},{9,13},{10,1... | collective-permute-start | bytes 786440 | tf_op jit(solution)/shard_map/ppermute | solution.py:190
  12.5 4.8 %collective-permute-start.3 = (bf16[128,1024]{1,0:T(8,128)(2,1)S(1)}, bf16[128,1024]{1,0:T(8,128)(2,1)S(1)}, u32[]{:S(2)}, u32[]{:S(2)}) collective-permute-start(bf16[128,1024]{1,0:T(8,128)(2,1)S(1)} %get-tuple-element.94), channel_id=1, source_target_pairs={{0,2},{1,6},{2,3},{3,7},{4,0},{5,4},{6,1},{7,5},{8,10},{9,14},{10,... | collective-permute-start | bytes 786440 | tf_op jit(solution)/shard_map/ppermute | solution.py:190
  17.4 2.6 %collective-permute-start.4 = (bf16[128,1024]{1,0:T(8,128)(2,1)S(1)}, bf16[128,1024]{1,0:T(8,128)(2,1)S(1)}, u32[]{:S(2)}, u32[]{:S(2)}) collective-permute-start(bf16[128,1024]{1,0:T(8,128)(2,1)S(1)} %get-tuple-element.91), channel_id=1, source_target_pairs={{0,3},{1,7},{2,0},{3,4},{4,1},{5,5},{6,2},{7,6},{8,11},{9,15},{10,... | collective-permute-start | bytes 786440 | tf_op jit(solution)/shard_map/ppermute | solution.py:190
  20.3 3.8 %collective-permute-start = (bf16[528,128]{1,0:T(8,128)(2,1)S(1)}, bf16[528,128]{1,0:T(8,128)(2,1)S(1)}, u32[]{:S(2)}, u32[]{:S(2)}) collective-permute-start(bf16[528,128]{1,0:T(8,128)(2,1)S(1)} %fusion.1.key_part), channel_id=1, source_target_pairs={{0,8},{8,16},{16,24},{24,32},{32,40},{40,48},{48,56},{1,9},{9,17},... | collective-permute-start | bytes 405512 | tf_op jit(solution)/shard_map/ppermute | solution.py:215
  24.1 5.0 %collective-permute-start.6 = (bf16[512,128]{1,0:T(8,128)(2,1)S(1)}, bf16[512,128]{1,0:T(8,128)(2,1)S(1)}, u32[]{:S(2)}, u32[]{:S(2)}) collective-permute-start(bf16[512,128]{1,0:T(8,128)(2,1)S(1)} %bitcast.47), channel_id=1, source_target_pairs={{0,8},{8,16},{16,24},{24,32},{32,40},{40,48},{48,56},{1,9},{9,17},... | collective-permute-start | bytes 393224 | tf_op jit(solution)/shard_map/ppermute | solution.py:215
  29.3 4.6 %attend.7 = (bf16[512,1024]{1,0:T(8,128)(2,1)S(1)}, f32[8,512]{1,0:T(8,128)S(1)}, f32[8,512]{1,0:T(8,128)S(1)}, f32[8,128,512]{2,1,0:T(8,128)S(1)}) custom-call(s32[3]{0:T(128)S(1)} %pad_add_fusion.place, f32[8,512]{1,0:T(8,128)S(1)} %broadcast_in_dim.21.query_docs, bf16[528,128]{1,0:T(8,128)(2,1)S(1)} %fusion.1.key_part, bf16[512,128]{1,0:T(8,128)(2,1)S(1)} %bitcast.48, ...), custom_call_target="tpu_custom_call" | custom-call | flops 1073741824 | bytes 5242880 | tf_op jit(solution)/shard_map/attend/pallas_call | solution.py:156
  33.9 3.8 %collective-permute-start.5 = (bf16[528,128]{1,0:T(8,128)(2,1)S(1)}, bf16[528,128]{1,0:T(8,128)(2,1)S(1)}, u32[]{:S(2)}, u32[]{:S(2)}) collective-permute-start(bf16[528,128]{1,0:T(8,128)(2,1)S(1)} %collective-permute-done.key_part), channel_id=1, source_target_pairs={{8,16},{16,24},{24,32},{32,40},{40,48},{48,56},{9,17},{17,25},{25,... | collective-permute-start | bytes 405512 | tf_op jit(solution)/shard_map/ppermute | solution.py:215
  37.7 3.8 %collective-permute-start.8 = (bf16[512,128]{1,0:T(8,128)(2,1)S(1)}, bf16[512,128]{1,0:T(8,128)(2,1)S(1)}, u32[]{:S(2)}, u32[]{:S(2)}) collective-permute-start(bf16[512,128]{1,0:T(8,128)(2,1)S(1)} %collective-permute-done.6.value_part), channel_id=1, source_target_pairs={{8,16},{16,24},{24,32},{32,40},{40,48},{48,56},{9,17},{17,25},{25,... | collective-permute-start | bytes 393224 | tf_op jit(solution)/shard_map/ppermute | solution.py:215
  41.5 0.8 attend.8
  42.4 7.0 %collective-permute-start.7 = (bf16[528,128]{1,0:T(8,128)(2,1)S(1)}, bf16[528,128]{1,0:T(8,128)(2,1)S(1)}, u32[]{:S(2)}, u32[]{:S(2)}) collective-permute-start(bf16[528,128]{1,0:T(8,128)(2,1)S(1)} %collective-permute-done.5.key_part), channel_id=1, source_target_pairs={{16,24},{24,32},{32,40},{40,48},{48,56},{17,25},{25,33},{33,41},{4... | collective-permute-start | bytes 405512 | tf_op jit(solution)/shard_map/ppermute | solution.py:215
  49.4 2.4 %collective-permute-start.10 = (bf16[512,128]{1,0:T(8,128)(2,1)S(1)}, bf16[512,128]{1,0:T(8,128)(2,1)S(1)}, u32[]{:S(2)}, u32[]{:S(2)}) collective-permute-start(bf16[512,128]{1,0:T(8,128)(2,1)S(1)} %collective-permute-done.8.value_part), channel_id=1, source_target_pairs={{16,24},{24,32},{32,40},{40,48},{48,56},{17,25},{25,33},{33,41},{4... | collective-permute-start | bytes 393224 | tf_op jit(solution)/shard_map/ppermute | solution.py:215
  51.8 0.8 attend.9
  53.3 1.9 %collective-permute-done.10.value_part = bf16[512,128]{1,0:T(8,128)(2,1)S(1)} collective-permute-done((bf16[512,128]{1,0:T(8,128)(2,1)S(1)}, bf16[512,128]{1,0:T(8,128)(2,1)S(1)}, u32[]{:S(2)}, u32[]{:S(2)}) %collective-permute-start.10) | collective-permute-done | bytes 131104 | tf_op jit(solution)/shard_map/ppermute | solution.py:215
  55.9 0.8 attend.10
  58.1 0.8 attend.11
  60.3 1.3 collective-permute-start.16
  61.6 1.0 attend.12
  62.6 40.5 %collective-permute-done.16.refs_4_ = bf16[16,128]{1,0:T(8,128)(2,1)S(1)} collective-permute-done((bf16[16,128]{1,0:T(8,128)(2,1)S(1)}, bf16[16,128]{1,0:T(8,128)(2,1)S(1)}, u32[]{:S(2)}, u32[]{:S(2)}) %collective-permute-start.16) | collective-permute-done | bytes 4128 | tf_op jit(solution)/shard_map/ppermute | solution.py:227
  103.1 1.9 %attend.13 = bf16[4,128,1024]{2,1,0:T(8,128)(2,1)S(1)} custom-call(s32[3]{0:T(128)S(1)} %pad_add_fusion.place, f32[8,512]{1,0:T(8,128)S(1)} %broadcast_in_dim.21.query_docs, bf16[528,128]{1,0:T(8,128)(2,1)S(1)} %collective-permute-done.13.key_part, bf16[512,128]{1,0:T(8,128)(2,1)S(1)} %collective-permute-done.15.value_part, ...), custom_call_target="tpu_custom_call" | custom-call | flops 1073741824 | bytes 5242880 | tf_op jit(solution)/shard_map/attend/pallas_call | solution.py:156
  105.1 1.9 %collective-permute-start.17 = (bf16[128,1024]{1,0:T(8,128)(2,1)S(1)}, bf16[128,1024]{1,0:T(8,128)(2,1)S(1)}, u32[]{:S(2)}, u32[]{:S(2)}) collective-permute-start(bf16[128,1024]{1,0:T(8,128)(2,1)S(1)} %get-tuple-element.87), channel_id=1, source_target_pairs={{0,64},{1,0},{2,68},{3,4},{4,65},{5,1},{6,69},{7,5},{64,128},{65,2... | collective-permute-start | bytes 786440 | tf_op jit(solution)/shard_map/ppermute | solution.py:245
  107.0 9.5 %collective-permute-start.18 = (bf16[128,1024]{1,0:T(8,128)(2,1)S(1)}, bf16[128,1024]{1,0:T(8,128)(2,1)S(1)}, u32[]{:S(2)}, u32[]{:S(2)}) collective-permute-start(bf16[128,1024]{1,0:T(8,128)(2,1)S(1)} %get-tuple-element.90), channel_id=1, source_target_pairs={{0,66},{1,2},{2,70},{3,6},{4,67},{5,3},{6,71},{7,7},{64,130},{65,4... | collective-permute-start | bytes 786440 | tf_op jit(solution)/shard_map/ppermute | solution.py:245
  116.5 4.4 %collective-permute-start.19 = (bf16[128,1024]{1,0:T(8,128)(2,1)S(1)}, bf16[128,1024]{1,0:T(8,128)(2,1)S(1)}, u32[]{:S(2)}, u32[]{:S(2)}) collective-permute-start(bf16[128,1024]{1,0:T(8,128)(2,1)S(1)} %get-tuple-element.89), channel_id=1, source_target_pairs={{0,68},{1,4},{2,64},{3,0},{4,69},{5,5},{6,65},{7,1},{64,132},{65,6... | collective-permute-start | bytes 786440 | tf_op jit(solution)/shard_map/ppermute | solution.py:245
  120.8 4.8 %collective-permute-start.20 = (bf16[128,1024]{1,0:T(8,128)(2,1)S(1)}, bf16[128,1024]{1,0:T(8,128)(2,1)S(1)}, u32[]{:S(2)}, u32[]{:S(2)}) collective-permute-start(bf16[128,1024]{1,0:T(8,128)(2,1)S(1)} %get-tuple-element.88), channel_id=1, source_target_pairs={{0,70},{1,6},{2,66},{3,2},{4,71},{5,7},{6,67},{7,3},{64,134},{65,0... | collective-permute-start | bytes 786440 | tf_op jit(solution)/shard_map/ppermute | solution.py:245
  125.7 16.8 %collective-permute-done.18 = bf16[128,1024]{1,0:T(8,128)(2,1)S(1)} collective-permute-done((bf16[128,1024]{1,0:T(8,128)(2,1)S(1)}, bf16[128,1024]{1,0:T(8,128)(2,1)S(1)}, u32[]{:S(2)}, u32[]{:S(2)}) %collective-permute-start.18) | collective-permute-done | bytes 262176 | tf_op jit(solution)/shard_map/ppermute | solution.py:245
  142.5 12.7 %collective-permute-done.19 = bf16[128,1024]{1,0:T(8,128)(2,1)S(1)} collective-permute-done((bf16[128,1024]{1,0:T(8,128)(2,1)S(1)}, bf16[128,1024]{1,0:T(8,128)(2,1)S(1)}, u32[]{:S(2)}, u32[]{:S(2)}) %collective-permute-start.19) | collective-permute-done | bytes 262176 | tf_op jit(solution)/shard_map/ppermute | solution.py:245
  155.2 28.0 %collective-permute-done.20 = bf16[128,1024]{1,0:T(8,128)(2,1)S(1)} collective-permute-done((bf16[128,1024]{1,0:T(8,128)(2,1)S(1)}, bf16[128,1024]{1,0:T(8,128)(2,1)S(1)}, u32[]{:S(2)}, u32[]{:S(2)}) %collective-permute-start.20) | collective-permute-done | bytes 262176 | tf_op jit(solution)/shard_map/ppermute | solution.py:245
  183.4 1.1 maximum_bitcast_fusion
  (44 shorter events, 5.0 us)
Async XLA Ops:
  0.0 7.4 %copy-start = (bf16[1,2,128,2048]{3,2,1,0:T(8,128)(2,1)S(1)}, bf16[1,2,128,2048]{3,2,1,0:T(8,128)(2,1)}, u32[]{:S(2)}) copy-start(bf16[1,2,128,2048]{3,2,1,0:T(8,128)(2,1)} %param.3) | copy-start | bytes 3145732
  2.7 17.4 %all-to-all-start = ((bf16[8,144,128]{2,1,0:T(8,128)(2,1)}), bf16[8,144,128]{2,1,0:T(8,128)(2,1)S(1)}, u32[]{:S(2)}, u32[]{:S(2)}) async-start(bf16[8,144,128]{2,1,0:T(8,128)(2,1)} %pad_maximum_fusion.1), calls=%async_computation | async-start | bytes 589824 | tf_op jit(solution)/shard_map/all_to_all | solution.py:199
  7.5 16.6 %collective-permute-start.1 = (bf16[128,1024]{1,0:T(8,128)(2,1)S(1)}, bf16[128,1024]{1,0:T(8,128)(2,1)S(1)}, u32[]{:S(2)}, u32[]{:S(2)}) collective-permute-start(bf16[128,1024]{1,0:T(8,128)(2,1)S(1)} %get-tuple-element.93), channel_id=1, source_target_pairs={{0,0},{1,4},{2,1},{3,5},{4,2},{5,6},{6,3},{7,7},{8,8},{9,12},{10,9... | collective-permute-start | bytes 786440 | tf_op jit(solution)/shard_map/ppermute | solution.py:190
  10.6 18.7 %collective-permute-start.2 = (bf16[128,1024]{1,0:T(8,128)(2,1)S(1)}, bf16[128,1024]{1,0:T(8,128)(2,1)S(1)}, u32[]{:S(2)}, u32[]{:S(2)}) collective-permute-start(bf16[128,1024]{1,0:T(8,128)(2,1)S(1)} %get-tuple-element.92), channel_id=1, source_target_pairs={{0,1},{1,5},{2,2},{3,6},{4,3},{5,7},{6,0},{7,4},{8,9},{9,13},{10,1... | collective-permute-start | bytes 786440 | tf_op jit(solution)/shard_map/ppermute | solution.py:190
  12.5 16.7 %collective-permute-start.3 = (bf16[128,1024]{1,0:T(8,128)(2,1)S(1)}, bf16[128,1024]{1,0:T(8,128)(2,1)S(1)}, u32[]{:S(2)}, u32[]{:S(2)}) collective-permute-start(bf16[128,1024]{1,0:T(8,128)(2,1)S(1)} %get-tuple-element.94), channel_id=1, source_target_pairs={{0,2},{1,6},{2,3},{3,7},{4,0},{5,4},{6,1},{7,5},{8,10},{9,14},{10,... | collective-permute-start | bytes 786440 | tf_op jit(solution)/shard_map/ppermute | solution.py:190
  17.4 11.9 %collective-permute-start.4 = (bf16[128,1024]{1,0:T(8,128)(2,1)S(1)}, bf16[128,1024]{1,0:T(8,128)(2,1)S(1)}, u32[]{:S(2)}, u32[]{:S(2)}) collective-permute-start(bf16[128,1024]{1,0:T(8,128)(2,1)S(1)} %get-tuple-element.91), channel_id=1, source_target_pairs={{0,3},{1,7},{2,0},{3,4},{4,1},{5,5},{6,2},{7,6},{8,11},{9,15},{10,... | collective-permute-start | bytes 786440 | tf_op jit(solution)/shard_map/ppermute | solution.py:190
  20.3 13.6 %collective-permute-start = (bf16[528,128]{1,0:T(8,128)(2,1)S(1)}, bf16[528,128]{1,0:T(8,128)(2,1)S(1)}, u32[]{:S(2)}, u32[]{:S(2)}) collective-permute-start(bf16[528,128]{1,0:T(8,128)(2,1)S(1)} %fusion.1.key_part), channel_id=1, source_target_pairs={{0,8},{8,16},{16,24},{24,32},{32,40},{40,48},{48,56},{1,9},{9,17},... | collective-permute-start | bytes 405512 | tf_op jit(solution)/shard_map/ppermute | solution.py:215
  24.1 13.6 %collective-permute-start.6 = (bf16[512,128]{1,0:T(8,128)(2,1)S(1)}, bf16[512,128]{1,0:T(8,128)(2,1)S(1)}, u32[]{:S(2)}, u32[]{:S(2)}) collective-permute-start(bf16[512,128]{1,0:T(8,128)(2,1)S(1)} %bitcast.47), channel_id=1, source_target_pairs={{0,8},{8,16},{16,24},{24,32},{32,40},{40,48},{48,56},{1,9},{9,17},... | collective-permute-start | bytes 393224 | tf_op jit(solution)/shard_map/ppermute | solution.py:215
  33.9 8.5 %collective-permute-start.5 = (bf16[528,128]{1,0:T(8,128)(2,1)S(1)}, bf16[528,128]{1,0:T(8,128)(2,1)S(1)}, u32[]{:S(2)}, u32[]{:S(2)}) collective-permute-start(bf16[528,128]{1,0:T(8,128)(2,1)S(1)} %collective-permute-done.key_part), channel_id=1, source_target_pairs={{8,16},{16,24},{24,32},{32,40},{40,48},{48,56},{9,17},{17,25},{25,... | collective-permute-start | bytes 405512 | tf_op jit(solution)/shard_map/ppermute | solution.py:215
  37.7 11.7 %collective-permute-start.8 = (bf16[512,128]{1,0:T(8,128)(2,1)S(1)}, bf16[512,128]{1,0:T(8,128)(2,1)S(1)}, u32[]{:S(2)}, u32[]{:S(2)}) collective-permute-start(bf16[512,128]{1,0:T(8,128)(2,1)S(1)} %collective-permute-done.6.value_part), channel_id=1, source_target_pairs={{8,16},{16,24},{24,32},{32,40},{40,48},{48,56},{9,17},{17,25},{25,... | collective-permute-start | bytes 393224 | tf_op jit(solution)/shard_map/ppermute | solution.py:215
  42.4 10.3 %collective-permute-start.7 = (bf16[528,128]{1,0:T(8,128)(2,1)S(1)}, bf16[528,128]{1,0:T(8,128)(2,1)S(1)}, u32[]{:S(2)}, u32[]{:S(2)}) collective-permute-start(bf16[528,128]{1,0:T(8,128)(2,1)S(1)} %collective-permute-done.5.key_part), channel_id=1, source_target_pairs={{16,24},{24,32},{32,40},{40,48},{48,56},{17,25},{25,33},{33,41},{4... | collective-permute-start | bytes 405512 | tf_op jit(solution)/shard_map/ppermute | solution.py:215
  49.4 5.9 %collective-permute-start.10 = (bf16[512,128]{1,0:T(8,128)(2,1)S(1)}, bf16[512,128]{1,0:T(8,128)(2,1)S(1)}, u32[]{:S(2)}, u32[]{:S(2)}) collective-permute-start(bf16[512,128]{1,0:T(8,128)(2,1)S(1)} %collective-permute-done.8.value_part), channel_id=1, source_target_pairs={{16,24},{24,32},{32,40},{40,48},{48,56},{17,25},{25,33},{33,41},{4... | collective-permute-start | bytes 393224 | tf_op jit(solution)/shard_map/ppermute | solution.py:215
  52.6 4.1 %collective-permute-start.9 = (bf16[528,128]{1,0:T(8,128)(2,1)S(1)}, bf16[528,128]{1,0:T(8,128)(2,1)S(1)}, u32[]{:S(2)}, u32[]{:S(2)}) collective-permute-start(bf16[528,128]{1,0:T(8,128)(2,1)S(1)} %collective-permute-done.7.key_part), channel_id=1, source_target_pairs={{24,32},{32,40},{40,48},{48,56},{25,33},{33,41},{41,49},{49,57},{2... | collective-permute-start | bytes 405512 | tf_op jit(solution)/shard_map/ppermute | solution.py:215
  55.3 2.2 %collective-permute-start.12 = (bf16[512,128]{1,0:T(8,128)(2,1)S(1)}, bf16[512,128]{1,0:T(8,128)(2,1)S(1)}, u32[]{:S(2)}, u32[]{:S(2)}) collective-permute-start(bf16[512,128]{1,0:T(8,128)(2,1)S(1)} %collective-permute-done.10.value_part), channel_id=1, source_target_pairs={{24,32},{32,40},{40,48},{48,56},{25,33},{33,41},{41,49},{49,57},{2... | collective-permute-start | bytes 393224 | tf_op jit(solution)/shard_map/ppermute | solution.py:215
  56.8 2.2 %collective-permute-start.11 = (bf16[528,128]{1,0:T(8,128)(2,1)S(1)}, bf16[528,128]{1,0:T(8,128)(2,1)S(1)}, u32[]{:S(2)}, u32[]{:S(2)}) collective-permute-start(bf16[528,128]{1,0:T(8,128)(2,1)S(1)} %collective-permute-done.9.key_part), channel_id=1, source_target_pairs={{32,40},{40,48},{48,56},{33,41},{41,49},{49,57},{34,42},{42,50},{5... | collective-permute-start | bytes 405512 | tf_op jit(solution)/shard_map/ppermute | solution.py:215
  57.4 2.2 %collective-permute-start.14 = (bf16[512,128]{1,0:T(8,128)(2,1)S(1)}, bf16[512,128]{1,0:T(8,128)(2,1)S(1)}, u32[]{:S(2)}, u32[]{:S(2)}) collective-permute-start(bf16[512,128]{1,0:T(8,128)(2,1)S(1)} %collective-permute-done.12.value_part), channel_id=1, source_target_pairs={{32,40},{40,48},{48,56},{33,41},{41,49},{49,57},{34,42},{42,50},{5... | collective-permute-start | bytes 393224 | tf_op jit(solution)/shard_map/ppermute | solution.py:215
  59.0 44.1 %collective-permute-start.13 = (bf16[528,128]{1,0:T(8,128)(2,1)S(1)}, bf16[528,128]{1,0:T(8,128)(2,1)S(1)}, u32[]{:S(2)}, u32[]{:S(2)}) collective-permute-start(bf16[528,128]{1,0:T(8,128)(2,1)S(1)} %collective-permute-done.11.key_part), channel_id=1, source_target_pairs={{40,48},{48,56},{41,49},{49,57},{42,50},{50,58},{43,51},{51,59},{4... | collective-permute-start | bytes 405512 | tf_op jit(solution)/shard_map/ppermute | solution.py:215
  59.6 43.5 %collective-permute-start.15 = (bf16[512,128]{1,0:T(8,128)(2,1)S(1)}, bf16[512,128]{1,0:T(8,128)(2,1)S(1)}, u32[]{:S(2)}, u32[]{:S(2)}) collective-permute-start(bf16[512,128]{1,0:T(8,128)(2,1)S(1)} %collective-permute-done.14.value_part), channel_id=1, source_target_pairs={{40,48},{48,56},{41,49},{49,57},{42,50},{50,58},{43,51},{51,59},{4... | collective-permute-start | bytes 393224 | tf_op jit(solution)/shard_map/ppermute | solution.py:215
  60.3 42.8 %collective-permute-start.16 = (bf16[16,128]{1,0:T(8,128)(2,1)S(1)}, bf16[16,128]{1,0:T(8,128)(2,1)S(1)}, u32[]{:S(2)}, u32[]{:S(2)}) collective-permute-start(bf16[16,128]{1,0:T(8,128)(2,1)S(1)} %slice.27), channel_id=1, source_target_pairs={{56,24},{48,16},{40,32},{57,25},{49,17},{41,33},{58,26},{50,18},{4... | collective-permute-start | bytes 12296 | tf_op jit(solution)/shard_map/ppermute | solution.py:227
  105.1 20.6 %collective-permute-start.17 = (bf16[128,1024]{1,0:T(8,128)(2,1)S(1)}, bf16[128,1024]{1,0:T(8,128)(2,1)S(1)}, u32[]{:S(2)}, u32[]{:S(2)}) collective-permute-start(bf16[128,1024]{1,0:T(8,128)(2,1)S(1)} %get-tuple-element.87), channel_id=1, source_target_pairs={{0,64},{1,0},{2,68},{3,4},{4,65},{5,1},{6,69},{7,5},{64,128},{65,2... | collective-permute-start | bytes 786440 | tf_op jit(solution)/shard_map/ppermute | solution.py:245
  107.0 35.5 %collective-permute-start.18 = (bf16[128,1024]{1,0:T(8,128)(2,1)S(1)}, bf16[128,1024]{1,0:T(8,128)(2,1)S(1)}, u32[]{:S(2)}, u32[]{:S(2)}) collective-permute-start(bf16[128,1024]{1,0:T(8,128)(2,1)S(1)} %get-tuple-element.90), channel_id=1, source_target_pairs={{0,66},{1,2},{2,70},{3,6},{4,67},{5,3},{6,71},{7,7},{64,130},{65,4... | collective-permute-start | bytes 786440 | tf_op jit(solution)/shard_map/ppermute | solution.py:245
  116.5 38.7 %collective-permute-start.19 = (bf16[128,1024]{1,0:T(8,128)(2,1)S(1)}, bf16[128,1024]{1,0:T(8,128)(2,1)S(1)}, u32[]{:S(2)}, u32[]{:S(2)}) collective-permute-start(bf16[128,1024]{1,0:T(8,128)(2,1)S(1)} %get-tuple-element.89), channel_id=1, source_target_pairs={{0,68},{1,4},{2,64},{3,0},{4,69},{5,5},{6,65},{7,1},{64,132},{65,6... | collective-permute-start | bytes 786440 | tf_op jit(solution)/shard_map/ppermute | solution.py:245
  120.8 62.3 %collective-permute-start.20 = (bf16[128,1024]{1,0:T(8,128)(2,1)S(1)}, bf16[128,1024]{1,0:T(8,128)(2,1)S(1)}, u32[]{:S(2)}, u32[]{:S(2)}) collective-permute-start(bf16[128,1024]{1,0:T(8,128)(2,1)S(1)} %get-tuple-element.88), channel_id=1, source_target_pairs={{0,70},{1,6},{2,66},{3,2},{4,71},{5,7},{6,67},{7,3},{64,134},{65,0... | collective-permute-start | bytes 786440 | tf_op jit(solution)/shard_map/ppermute | solution.py:245
